TPU v7x, 256 devices: a whole 4x4x8 slice. The times are simulated.
256 devices in a mesh: clip: 16 (over x, z_hi), seq: 16 (over y, z_lo, core).
Axes of the slice: x: 4, y: 4, z: 8 (z_hi: 4, z_lo: 2; z = z_hi * 2 + z_lo), core: 2. Of those that a mesh axis runs over, the one named last changes fastest.
Arguments:
- tokens: bfloat16 [16, 8192, 768], P('clip', 'seq'), may hold values from -6 to 6
- out_grad: bfloat16 [16, 8192, 768], P('clip', 'seq'), may hold values from -6144 to 6144
- saved_logits: bfloat16 [16, 8192, 1024], P('clip', 'seq'), may hold values from -14 to 400
- slot_params: bfloat16 [768, 1024], P(None, 'seq'), may hold values from -0.21875 to 0.21875
- slot_inputs: bfloat16 [16, 1024, 768], P(None, ('clip', 'seq')), may hold values from -6 to 6
- slot_outputs: bfloat16 [16, 1024, 768], P('clip', 'seq'), may hold values from -0.119628906 to 0.119628906
- expert_in: bfloat16 [256, 768, 3072], P(('clip', 'seq')), may hold values from -0.21875 to 0.21875
- expert_out: bfloat16 [256, 3072, 768], P(('clip', 'seq')), may hold values from -0.109375 to 0.109375
Outputs:
- token_grad: bfloat16 [16, 8192, 768], P('clip', 'seq')
All inputs are finite; a program needn't handle non-finite values.
Results may differ from a plain program's by a relative error of at most 0.023.
Values may be sent and summed in bfloat16 or wider, within the bound.
A program may use at most 64 MiB of HBM per device.

v0:
```python
import jax
import jax.numpy as jnp
from jax import lax
from jax.sharding import PartitionSpec as P


def combined_all(value, axis, join):
    pieces = jax.tree.map(lambda part: lax.all_gather(part, axis), value)
    head = jax.tree.map(lambda part: part[0], pieces)
    tail = jax.tree.map(lambda part: part[1:], pieces)
    total, _ = lax.scan(lambda total, piece: (join(total, piece), None), head, tail)
    return total


def merge_stats(first, second):
    highest = jnp.maximum(first[0], second[0])
    total = first[1] * jnp.exp(first[0] - highest) + second[1] * jnp.exp(second[0] - highest)
    return (highest, total)


def on_device(
    tokens, out_grad, saved_logits, slot_params, slot_inputs, slot_outputs, expert_in, expert_out
):
    clip_count = lax.axis_size("clip")
    seq_count = lax.axis_size("seq")
    tok_feats = tokens[0]
    out_cot = out_grad[0]
    scores = saved_logits[0].astype(jnp.float32)
    width = tok_feats.shape[1]
    slot_total = scores.shape[1]
    clip_total = slot_inputs.shape[0]
    local_slots = slot_inputs.shape[1]
    expert_block = expert_in.shape[0]
    slot_each = local_slots // expert_block
    param_all, outputs_all = (
        lax.all_gather(slot_params, "seq", axis=1, tiled=True),
        lax.all_gather(slot_outputs, "seq", axis=1, tiled=True),
    )
    slot_out = outputs_all[0]
    combine = jax.nn.softmax(scores, axis=1)
    local_max = jnp.max(scores, axis=0)
    local_sum = jnp.sum(jnp.exp(scores - local_max), axis=0)
    col_max, col_sum = combined_all((local_max, local_sum), "seq", merge_stats)
    dispatch = jnp.exp(scores - col_max) / col_sum
    comb_cot = jnp.einsum("td,sd->ts", out_cot, slot_out, preferred_element_type=jnp.float32)
    comb_logit = combine * (comb_cot - jnp.sum(combine * comb_cot, axis=1, keepdims=True))
    partial_cot = jnp.einsum(
        "ts,td->sd", combine.astype(jnp.bfloat16), out_cot, preferred_element_type=jnp.float32
    )
    summed = lax.psum(partial_cot.astype(jnp.bfloat16), "seq")
    blocks = summed.reshape(clip_count, seq_count, local_slots, width)
    mine = lax.dynamic_index_in_dim(blocks, lax.axis_index("seq"), 1, keepdims=False)
    received = lax.all_to_all(mine, "clip", split_axis=0, concat_axis=0, tiled=True)
    expert_cot = received.reshape(clip_total, expert_block, slot_each, width)
    expert_feed = slot_inputs.reshape(clip_total, expert_block, slot_each, width)
    hidden = jnp.einsum(
        "cejd,edh->cejh", expert_feed, expert_in, preferred_element_type=jnp.float32
    )
    act_cot = jnp.einsum(
        "cejd,ehd->cejh", expert_cot, expert_out, preferred_element_type=jnp.float32
    )
    unused, pull_back = jax.vjp(jax.nn.gelu, hidden)
    hidden_cot = pull_back(act_cot)[0].astype(jnp.bfloat16)
    local_grad = jnp.einsum(
        "cejh,edh->cejd", hidden_cot, expert_in, preferred_element_type=jnp.float32
    )
    local_grad = local_grad.astype(jnp.bfloat16)
    returned = lax.all_to_all(local_grad, "clip", split_axis=0, concat_axis=0, tiled=True)
    collected = lax.all_gather(returned, "seq", axis=1, tiled=True)
    slot_grad = collected.reshape(slot_total, width)
    dispatch_b = dispatch.astype(jnp.bfloat16)
    direct = jnp.dot(dispatch_b, slot_grad, preferred_element_type=jnp.float32)
    disp_cot = jnp.einsum("td,sd->ts", tok_feats, slot_grad, preferred_element_type=jnp.float32)
    slot_dots = lax.psum(jnp.sum(dispatch * disp_cot, axis=0), "seq")
    disp_logit = dispatch * (disp_cot - slot_dots)
    logit_grad = (comb_logit + disp_logit).astype(jnp.bfloat16)
    through = jnp.einsum("ts,ds->td", logit_grad, param_all, preferred_element_type=jnp.float32)
    return (direct + through).astype(jnp.bfloat16)[None]


def solution(mesh):
    placed = (
        P("clip", "seq", None),
        P("clip", "seq", None),
        P("clip", "seq", None),
        P(None, "seq"),
        P(None, ("clip", "seq"), None),
        P("clip", "seq", None),
        P(("clip", "seq"), None, None),
        P(("clip", "seq"), None, None),
    )
    return jax.shard_map(
        on_device, mesh=mesh, in_specs=placed, out_specs=P("clip", "seq", None), check_vma=False
    )
```

profile of v0, /device:TPU:1, one launch (start us, length us, event | category | flops | bytes accessed | tf_op | source)
XLA Modules:
  0.0 301.7 jit_solution(11144078357363737986)
XLA Ops:
  6.5 1.8 fusion.84
  8.4 2.0 fusion.16
  10.4 1.2 convolution_convert_fusion
  11.7 1.4 reshape.71
  13.0 130.9 %all-reduce.2.cloned.1.call-done = bf16[16,16,4,768]{3,2,1,0:T(4,128)(2,1)} async-done(((bf16[16,16,4,768]{3,2,1,0:T(4,128)(2,1)}), bf16[16,16,4,768]{3,2,1,0:T(4,128)(2,1)}) %all-reduce.2.cloned.1.call-update) | async-done | bytes 1572880 | tf_op jit(solution)/shard_map/psum | solution.py:50
  144.0 1.6 dynamic-slice_bitcast_fusion
  145.6 8.4 %all-to-all-start = ((bf16[16,4,768]{2,1,0:T(4,128)(2,1)}), bf16[16,4,768]{2,1,0:T(4,128)(2,1)S(1)}, u32[]{:S(2)}, u32[]{:S(2)}) async-start(bf16[16,4,768]{2,1,0:T(4,128)(2,1)} %dynamic-slice_bitcast_fusion), calls=%async_computation | async-start | bytes 196608 | tf_op jit(solution)/shard_map/all_to_all | solution.py:53
  154.0 3.3 %fusion.9 = f32[16,1,4,3072]{3,0,2,1:T(8,128)S(1)} fusion(bf16[1,768,3072]{2,1,0:T(8,128)(2,1)} %param.16, bf16[16,4,768]{2,1,0:T(4,128)(2,1)S(1)} %copy-done.3), kind=kOutput, calls=%fused_computation.10 | convolution fusion | flops 301989888 | bytes 5603328 | tf_op jit(solution)/shard_map/cejd,edh->cejh/dot_general | solution.py:56
  157.3 6.0 %all-to-all-done = bf16[16,4,768]{2,1,0:T(4,128)(2,1)S(1)} async-done(((bf16[16,4,768]{2,1,0:T(4,128)(2,1)}), bf16[16,4,768]{2,1,0:T(4,128)(2,1)S(1)}, u32[]{:S(2)}, u32[]{:S(2)}) %all-to-all-start) | async-done | bytes 98336 | tf_op jit(solution)/shard_map/all_to_all | solution.py:53
  163.3 6.8 %fusion.38 = bf16[16,1,4,768]{3,0,2,1:T(8,128)(2,1)S(1)} fusion(bf16[1,768,3072]{2,1,0:T(8,128)(2,1)} %param.16, f32[16,1,4,3072]{3,0,2,1:T(8,128)S(1)} %fusion.9, bf16[1,3072,768]{2,1,0:T(8,128)(2,1)} %param.17, bf16[16,4,768]{2,1,0:T(4,128)(2,1)S(1)} %all-to-all-done), kind=kOutput, calls=%fused_computation.45 | convolution fusion | flops 607961088 | bytes 10420224 | tf_op jit(solution)/shard_map/cejh,edh->cejd/dot_general | solution.py:64
  170.2 12.2 %all_to_all.10 = bf16[16,1,4,768]{3,2,1,0:T(4,128)(2,1)S(1)} all-to-all(bf16[16,1,4,768]{3,2,1,0:T(4,128)(2,1)S(1)} %copy.16), channel_id=1, replica_groups=mesh['clip'=16,'seq'=16] {'clip'}, dimensions={0} | all-to-all | bytes 196608 | tf_op jit(solution)/shard_map/all_to_all | solution.py:68
  183.1 0.7 all-gather.8.cloned.1.call-update
  184.3 20.2 %all-gather.1 = f32[16384]{0:T(1024)S(1)} all-gather(f32[1024]{0:T(1024)S(1)} %get-tuple-element.37), channel_id=3, replica_groups=mesh['clip'=16,'seq'=16] {'seq'}, dimensions={0}, use_global_device_ids=true | all-gather | bytes 69632 | tf_op jit(solution)/shard_map/all_gather | solution.py:8
  204.5 17.6 %all-gather = f32[16384]{0:T(1024)S(1)} all-gather(f32[1024]{0:T(1024)S(1)} %reduce_max.38), channel_id=2, replica_groups=mesh['clip'=16,'seq'=16] {'seq'}, dimensions={0}, use_global_device_ids=true | all-gather | bytes 69632 | tf_op jit(solution)/shard_map/all_gather | solution.py:8
  222.1 0.8 while.12
  223.0 2.2 copy.18
  225.2 1.4 reshape.75
  226.6 4.0 %fusion.58 = f32[1024,512]{0,1:T(8,128)} fusion(bf16[1024,768]{1,0:T(8,128)(2,1)} %reshape.75, bf16[1,512,768]{2,1,0:T(8,128)(2,1)} %param.10), kind=kOutput, calls=%fused_computation.60 | convolution fusion | flops 805306368 | bytes 4456448 | tf_op jit(solution)/shard_map/td,sd->ts/dot_general | solution.py:73
  230.6 21.3 %all-gather.8.cloned.1.call-done = bf16[1,1024,768]{2,1,0:T(8,128)(2,1)} async-done(((bf16[1,64,768]{2,1,0:T(8,128)(2,1)}), bf16[1,1024,768]{2,1,0:T(8,128)(2,1)}) %all-gather.8.cloned.1.call-update) | async-done | bytes 1572880 | tf_op jit(solution)/shard_map/all_gather | solution.py:37
  251.9 4.9 %multiply_reduce_fusion = (f32[512]{0:T(512)S(1)}, f32[1024]{0:T(1024)S(1)}, f32[512,1024]{1,0:T(8,128)}) fusion(bf16[1,512,1024]{2,1,0:T(8,128)(2,1)S(1)} %copy-done.2, f32[512]{0:T(512)S(1)} %get-tuple-element.38, f32[512]{0:T(512)S(1)} %reduce_max.37, f32[1024,512]{0,1:T(8,128)} %fusion.58, f32[1024]{0:T(1024)S(1)} %get-tuple-element.34, ...), kind=kOutput, calls=%fused_computation.36 | convolution fusion | flops 810023424 | bytes 7620608 | tf_op jit(solution)/shard_map/td,sd->ts/dot_general | solution.py:45
  256.8 27.0 %psum.15 = f32[1024]{0:T(1024)S(1)} all-reduce(f32[1024]{0:T(1024)S(1)} %get-tuple-element.36), channel_id=1, replica_groups=mesh['clip'=16,'seq'=16] {'seq'}, use_global_device_ids=true, to_apply=%region_9.10 | all-reduce | flops 1024 | bytes 8192 | tf_op jit(solution)/shard_map/psum | solution.py:74
  283.9 2.3 fusion.44
  286.1 3.2 %all-gather.10.cloned.1.call-done = bf16[768,1024]{0,1:T(8,128)(2,1)} async-done(((bf16[768,64]{0,1:T(8,128)(2,1)}), bf16[768,1024]{0,1:T(8,128)(2,1)}) %all-gather.10.cloned.1.call-update) | async-done | bytes 1572880 | tf_op jit(solution)/shard_map/all_gather | solution.py:36
  289.3 5.8 %fusion.34 = bf16[1,512,768]{2,1,0:T(8,128)(2,1)} fusion(f32[512,768]{1,0:T(8,128)} %fusion.44, bf16[768,1024]{0,1:T(8,128)(2,1)} %all-gather.10.cloned.1.call-done, f32[1024,512]{0,1:T(8,128)} %fusion.58, f32[512,1024]{1,0:T(8,128)} %get-tuple-element.55, bf16[1,512,1024]{2,1,0:T(8,128)(2,1)S(1)} %copy-done.2, f32[1024]{0:T(1024)S(1)} %psum.15, ...), kind=kOutput, calls=%fused_computation.41 | convolution fusion | flops 811859968 | bytes 9193472 | tf_op jit(solution)/shard_map/ts,ds->td/dot_general | solution.py:77
  (56 shorter events, 1.9 us)
Async XLA Ops:
  6.5 3.9 %copy-start = (bf16[1,512,768]{2,1,0:T(8,128)(2,1)S(1)}, bf16[1,512,768]{2,1,0:T(8,128)(2,1)}, u32[]{:S(2)}) copy-start(bf16[1,512,768]{2,1,0:T(8,128)(2,1)} %param.11) | copy-start | bytes 2359300
  6.5 3.9 %copy-start.2 = (bf16[1,512,1024]{2,1,0:T(8,128)(2,1)S(1)}, bf16[1,512,1024]{2,1,0:T(8,128)(2,1)}, u32[]{:S(2)}) copy-start(bf16[1,512,1024]{2,1,0:T(8,128)(2,1)} %param.12) | copy-start | bytes 3145732
  6.5 137.4 %all-reduce.2.cloned.1.call-start = ((), (), s32[]{:S(2)}) async-start(), calls=%async_computation.2 | async-start | bytes 3145728 | tf_op jit(solution)/shard_map/psum | solution.py:50
  11.6 142.4 %copy-start.3 = (bf16[16,4,768]{2,1,0:T(4,128)(2,1)S(1)}, bf16[16,4,768]{2,1,0:T(4,128)(2,1)}, u32[]{:S(2)}) copy-start(bf16[16,4,768]{2,1,0:T(4,128)(2,1)} %param.14) | copy-start | bytes 294916
  145.6 17.8 %all-to-all-start = ((bf16[16,4,768]{2,1,0:T(4,128)(2,1)}), bf16[16,4,768]{2,1,0:T(4,128)(2,1)S(1)}, u32[]{:S(2)}, u32[]{:S(2)}) async-start(bf16[16,4,768]{2,1,0:T(4,128)(2,1)} %dynamic-slice_bitcast_fusion), calls=%async_computation | async-start | bytes 196608 | tf_op jit(solution)/shard_map/all_to_all | solution.py:53
  153.9 69.0 %all-gather.6.cloned.1.call-start = ((), (), s32[]{:S(2)}) async-start(), calls=%async_computation.3 | async-start | bytes 1671168 | tf_op jit(solution)/shard_map/all_gather | solution.py:69
  183.0 68.9 %all-gather.8.cloned.1.call-start = ((), (), s32[]{:S(2)}) async-start(), calls=%async_computation.4 | async-start | bytes 1671168 | tf_op jit(solution)/shard_map/all_gather | solution.py:37
  183.8 105.6 %all-gather.10.cloned.1.call-start = ((), (), s32[]{:S(2)}) async-start(), calls=%async_computation.5 | async-start | bytes 1671168 | tf_op jit(solution)/shard_map/all_gather | solution.py:36
  251.9 31.9 %copy-start.1 = (bf16[1024,768]{1,0:T(8,128)(2,1)S(1)}, bf16[1024,768]{1,0:T(8,128)(2,1)}, u32[]{:S(2)}) copy-start(bf16[1024,768]{1,0:T(8,128)(2,1)} %reshape.75) | copy-start | bytes 4718596
Sparse Core Ops, SparseCore 0:
  13.2 130.7 all-reduce.1
  183.1 31.2 all-gather.5
  216.3 35.5 all-gather.7
  253.6 35.6 all-gather.9
where the time goes:
time: 302 us
  waiting for transfers between devices  163 us (54%)
  blocking collectives  77 us (25%)
  matrix products  28.2 us (9%)
  between operations  13.3 us (4%)
  starting transfers between devices  8.51 us (3%)
  local copies, waits for them, and re-layouts  7.55 us (2%)
  other arithmetic  4.06 us (1%)
    psum x1, waiting for transfers between devices, on_device(): summed = lax.psum(partial_cot.astype(jnp.bfloat16), 'seq')  131 us
    all_gather x2, blocking collectives, combined_all(): pieces = jax.tree.map(lambda part: lax.all_gather(part, axis), value)  37.7 us
    psum x1, blocking collectives, on_device(): slot_dots = lax.psum(jnp.sum(dispatch * disp_cot, axis=0), 'seq')  27 us
    all_gather x1, waiting for transfers between devices, on_device(): lax.all_gather(slot_outputs, 'seq', axis=1, tiled=True)  21.3 us
    all_to_all x1, blocking collectives, on_device(): lax.all_to_all(local_grad, 'clip', split_axis=0, concat_axis=0, tiled=True)  12.2 us
    all_to_all x1, starting transfers between devices, on_device(): lax.all_to_all(mine, 'clip', split_axis=0, concat_axis=0, tiled=True)  8.39 us
    dot_general x1, matrix products, on_device(): jnp.einsum('cejh,edh->cejd', hidden_cot, expert_in, preferred_element_typ...  6.78 us
  transfers between devices with their start and end apart: 5, of which 4 were waited for; matrix products, arithmetic and copies ran while one was open for 6% of the time, Pallas kernels for 0%

commit v1 on v0

v1 whole, which is shorter than its diff:
```python
import jax
import jax.numpy as jnp
from jax import lax
from jax.experimental import pallas as pl
from jax.experimental.pallas import tpu as pltpu
from jax.sharding import PartitionSpec as P

F32 = jnp.float32
BF16 = jnp.bfloat16
MESH = pl.DeviceIdType.MESH
NT = (((1,), (1,)), ((), ()))
TN = (((0,), (0,)), ((), ()))


def gelu_slope(x):
    k = 0.7978845608028654
    t = jnp.tanh(k * (x + 0.044715 * x * x * x))
    return 0.5 * (1.0 + t) + 0.5 * x * (1.0 - t * t) * (k * (1.0 + 0.134145 * x * x))


def kernel(
    tok_h, og_h, lg_h, pt_h, xin_h, so_h, win_h, wout_h, out_ref,
    lg, og, tok, win, wout, xin, cf, cb, pb, rp, hb, ry, st, qf, a2s, a2r, xf, gp, b2s, b2r, zf, sgb,
    ob, ptb, cc, ddf, dspf, dspb, stl, stb, dtl, dtb, acc,
    ld, cs_s, cs_r, y_s, y_r, a_s, a_r, b_s, b_r, g_s, g_r, k_s, k_r, o_s, o_r, p_s, p_r, st_s, st_r, dt_s, dt_r,
):
    c = lax.axis_index("clip")
    s = lax.axis_index("seq")
    y, q, h = s // 4, s % 4, s % 2
    zl = q // 2
    yr, y2, yl = (y + 1) % 4, (y + 2) % 4, (y + 3) % 4
    right, left = (c, yr * 4 + q), (c, yl * 4 + q)
    mate = (c, s + 1 - 2 * h)
    zmate = (c, s + 2 - 4 * zl)
    mine = pl.ds(pl.multiple_of(h * 384, 128), 384)
    other = pl.ds(pl.multiple_of((1 - h) * 384, 128), 384)

    def rows_of(yy):
        return pl.ds(pl.multiple_of(yy * 16, 16), 16)

    def remote(src, dst, ssem, rsem, dev):
        return pltpu.make_async_remote_copy(
            src_ref=src, dst_ref=dst, send_sem=ssem, recv_sem=rsem, device_id=dev, device_id_type=MESH
        )

    def plane(i):
        return ((c + i // 4) % 16, y * 4 + (q + i % 4) % 4)

    def group(i):
        return (c, (s + i) % 16)

    loads = [
        pltpu.make_async_copy(lg_h.at[0], lg, ld.at[0]),
        pltpu.make_async_copy(og_h.at[0], og, ld.at[1]),
        pltpu.make_async_copy(so_h.at[0], ob.at[y, zl, h], ld.at[2]),
        pltpu.make_async_copy(pt_h, ptb.at[y, zl, h], ld.at[3]),
        pltpu.make_async_copy(xin_h, xin, ld.at[4]),
        pltpu.make_async_copy(win_h.at[0], win, ld.at[5]),
        pltpu.make_async_copy(wout_h.at[0], wout, ld.at[6]),
        pltpu.make_async_copy(tok_h.at[0], tok, ld.at[7]),
    ]
    for load in loads:
        load.start()

    barrier = pltpu.get_barrier_semaphore()

    def greet_plane(i, carry):
        pl.semaphore_signal(barrier, inc=1, device_id=plane(i), device_id_type=MESH)
        return carry

    def greet_group(i, carry):
        pl.semaphore_signal(
            barrier, inc=1, device_id=(c, ((y + 1 + i // 4) % 4) * 4 + i % 4), device_id_type=MESH
        )
        return carry

    lax.fori_loop(0, 12, greet_group, 0)
    lax.fori_loop(1, 64, greet_plane, 0)

    loads[0].wait()

    def front(i, carry):
        rows = pl.ds(pl.multiple_of(i * 64, 64), 64)
        l = lg[rows, :].astype(F32)
        e = jnp.exp(l - jnp.max(l, axis=1, keepdims=True))
        comb = e * (1.0 / jnp.sum(e, axis=1, keepdims=True))
        cf[rows, :] = comb
        cb[rows, :] = comb.astype(BF16)
        return carry

    lax.fori_loop(0, 8, front, 0)
    loads[1].wait()
    pl.semaphore_wait(barrier, 75)

    def cs_copy(k):
        part = pl.ds(k * 4, 4)
        return remote(pb.at[part, :, other], rp.at[part], cs_s.at[k], cs_r.at[k], mate)

    def partial(k, carry):
        cols = pl.ds(pl.multiple_of(k * 256, 256), 256)
        p = lax.dot_general(cb[:, cols], og[...], TN, preferred_element_type=F32)
        pb[pl.ds(k * 4, 4)] = p.astype(BF16).reshape(4, 64, 768)
        cs_copy(k).start()
        return carry

    lax.fori_loop(0, 4, partial, 0)

    loads[2].wait()
    loads[3].wait()
    z_o = remote(ob.at[y, zl, h], ob.at[y, zl, h], o_s.at[0], o_r.at[0], zmate)
    z_p = remote(ptb.at[y, zl, h], ptb.at[y, zl, h], p_s.at[0], p_r.at[0], zmate)
    z_o.start()
    z_p.start()

    def half_sum(k, carry):
        part = pl.ds(k * 4, 4)
        cs_copy(k).wait_recv()
        hb[part] = (pb[part, :, mine].astype(F32) + rp[part].astype(F32)).astype(BF16)
        return carry

    lax.fori_loop(0, 4, half_sum, 0)

    A, B = pl.ds(0, 8), pl.ds(8, 8)

    def y_copy(i, src, dev):
        return remote(src, ry.at[i], y_s.at[i], y_r.at[i], dev)

    ys = [
        y_copy(0, hb.at[A, rows_of(y2)], right),
        y_copy(1, hb.at[B, rows_of(y2)], left),
        y_copy(2, hb.at[B, rows_of(yr)], right),
        y_copy(3, hb.at[A, rows_of(yl)], left),
        y_copy(4, st.at[0], right),
        y_copy(5, st.at[1], left),
    ]
    for i in range(4):
        ys[i].start()

    loads[4].wait()
    loads[5].wait()
    for i in range(16):
        xf[4 * i : 4 * i + 4, :] = xin[i].astype(F32)
    xin_b = xf[...].astype(BF16)

    def slope(i, carry):
        cols = pl.ds(pl.multiple_of(i * 512, 512), 512)
        hid = jnp.dot(xin_b, win[:, cols], preferred_element_type=F32)
        gp[:, cols] = gelu_slope(hid)
        return carry

    lax.fori_loop(0, 6, slope, 0)

    ys[0].wait_recv()
    st[0] = (ry[0].astype(F32) + hb[A, rows_of(yr), :].astype(F32)).astype(BF16)
    ys[4].start()
    ys[1].wait_recv()
    st[1] = (ry[1].astype(F32) + hb[B, rows_of(yl), :].astype(F32)).astype(BF16)
    ys[5].start()

    def gather(buf, ss, rs):
        return [
            remote(buf.at[y, :, h], buf.at[y, :, h], ss.at[1], rs.at[1], right),
            remote(buf.at[y, :, h], buf.at[y, :, h], ss.at[2], rs.at[2], left),
            remote(buf.at[yl, 0, h], buf.at[yl, 0, h], ss.at[3], rs.at[3], right),
            remote(buf.at[yr, 1, h], buf.at[yr, 1, h], ss.at[4], rs.at[4], left),
            remote(buf.at[:, :, h], buf.at[:, :, h], ss.at[5], rs.at[5], mate),
        ]

    o_g = gather(ob, o_s, o_r)
    p_g = gather(ptb, p_s, p_r)
    z_o.wait_recv()
    o_g[0].start()
    o_g[1].start()

    def colmax(i, m):
        rows = pl.ds(pl.multiple_of(i * 64, 64), 64)
        return jnp.maximum(m, jnp.max(lg[rows, :].astype(F32), axis=0, keepdims=True))

    m_loc = lax.fori_loop(1, 8, colmax, jnp.max(lg[0:64, :].astype(F32), axis=0, keepdims=True))

    def colsum(i, t):
        rows = pl.ds(pl.multiple_of(i * 64, 64), 64)
        return t + jnp.sum(jnp.exp(lg[rows, :].astype(F32) - m_loc), axis=0, keepdims=True)

    s_loc = lax.fori_loop(0, 8, colsum, jnp.zeros((1, 1024), F32))
    stl[0:1, :] = m_loc
    stl[1:2, :] = s_loc

    def st_copy(i):
        return remote(stl, stb.at[s], st_s.at[0], st_r.at[0], group(i))

    own_st = pltpu.make_async_copy(stl, stb.at[s], st_r.at[0])
    own_st.start()

    def st_start(i, carry):
        st_copy(i).start()
        return carry

    lax.fori_loop(1, 16, st_start, 0)

    ys[3].wait_recv()
    ys[4].wait_recv()
    qf[0:8] = hb[A, rows_of(y), :].astype(F32) + ry[3].astype(F32) + ry[4].astype(F32)
    ys[2].wait_recv()
    ys[5].wait_recv()
    qf[8:16] = hb[B, rows_of(y), :].astype(F32) + ry[2].astype(F32) + ry[5].astype(F32)
    for i in range(4):
        a2s[:, i] = qf[:, 4 * i : 4 * i + 4, :].astype(BF16)

    def a_start(i, carry):
        cd, sd = plane(i)
        remote(a2s.at[cd, sd % 4], a2r.at[c * 4 + q], a_s.at[0], a_r.at[0], (cd, sd)).start()
        return carry

    pltpu.make_async_copy(a2s.at[c, q], a2r.at[c * 4 + q], a_r.at[0]).start()
    lax.fori_loop(1, 64, a_start, 0)

    z_p.wait_recv()
    p_g[0].start()
    p_g[1].start()
    o_g[0].wait_recv()
    o_g[2].start()
    o_g[1].wait_recv()
    o_g[3].start()

    pltpu.make_async_copy(stb, stb, st_r.at[0]).wait()
    m_all = stb[:, 0, :]
    top = jnp.max(m_all, axis=0, keepdims=True)
    total = jnp.sum(stb[:, 1, :] * jnp.exp(m_all - top), axis=0, keepdims=True)
    inv_total = 1.0 / total

    def disp(i, carry):
        rows = pl.ds(pl.multiple_of(i * 64, 64), 64)
        d = jnp.exp(lg[rows, :].astype(F32) - top) * inv_total
        dspf[rows, :] = d
        dspb[rows, :] = d.astype(BF16)
        return carry

    lax.fori_loop(0, 8, disp, 0)

    loads[6].wait()
    pltpu.make_async_copy(a2r, a2r, a_r.at[0]).wait()
    for i in range(16):
        for j in range(2):
            xf[4 * i : 4 * i + 4, 384 * j : 384 * j + 384] = (
                a2r[4 * i + j].astype(F32) + a2r[4 * i + 2 + j].astype(F32)
            )
    x_b = xf[...].astype(BF16)
    xf[...] = jnp.zeros((64, 768), F32)

    def expert(i, carry):
        part = pl.ds(pl.multiple_of(i * 512, 512), 512)
        act = lax.dot_general(x_b, wout[part, :], NT, preferred_element_type=F32)
        hc = (act * gp[:, part]).astype(BF16)
        xf[...] += lax.dot_general(hc, win[:, part], NT, preferred_element_type=F32)
        return carry

    lax.fori_loop(0, 6, expert, 0)
    for i in range(16):
        for j in range(2):
            b2s[i, j] = xf[4 * i : 4 * i + 4, 384 * j : 384 * j + 384].astype(BF16)

    def b_start(i, carry):
        cd, sd = plane(i)
        remote(b2s.at[cd, sd % 2], b2r.at[c * 4 + q], b_s.at[0], b_r.at[0], (cd, sd)).start()
        return carry

    pltpu.make_async_copy(b2s.at[c, h], b2r.at[c * 4 + q], b_r.at[0]).start()
    lax.fori_loop(1, 64, b_start, 0)

    o_g[2].wait_recv()
    o_g[3].wait_recv()
    o_g[4].start()
    p_g[0].wait_recv()
    p_g[2].start()
    p_g[1].wait_recv()
    p_g[3].start()
    o_g[4].wait_recv()

    def comb_dot(i, carry):
        cols = pl.ds(pl.multiple_of(i * 256, 256), 256)
        w = ob[i].reshape(256, 768)
        cc[:, cols] = lax.dot_general(og[...], w, NT, preferred_element_type=F32)
        return carry

    lax.fori_loop(0, 4, comb_dot, 0)

    def comb_grad(i, carry):
        rows = pl.ds(pl.multiple_of(i * 64, 64), 64)
        comb = cf[rows, :]
        v = cc[rows, :]
        cc[rows, :] = comb * (v - jnp.sum(comb * v, axis=1, keepdims=True))
        return carry

    lax.fori_loop(0, 8, comb_grad, 0)
    p_g[2].wait_recv()
    p_g[3].wait_recv()
    p_g[4].start()

    loads[7].wait()
    pltpu.make_async_copy(b2r, b2r, b_r.at[0]).wait()
    back = b2r[...].reshape(16, 4, 4, 384)
    for i in range(4):
        zf[:, 4 * i : 4 * i + 4, :] = back[:, i].astype(F32)
    sgb[:, rows_of(y), mine] = zf[...].astype(BF16)

    def g_copy(i, part, yy, dev):
        ref = sgb.at[part, rows_of(yy), mine]
        return remote(ref, ref, g_s.at[i], g_r.at[i], dev)

    def k_copy(i, part, yy):
        ref = sgb.at[part, rows_of(yy), mine]
        return remote(ref, ref, k_s.at[i], k_r.at[i], mate)

    gs = [
        g_copy(0, A, y, right),
        g_copy(1, B, y, left),
        g_copy(2, B, y, right),
        g_copy(3, A, y, left),
        g_copy(4, A, yl, right),
        g_copy(5, B, yr, left),
    ]
    ks = [
        k_copy(0, A, y),
        k_copy(1, B, y),
        k_copy(2, A, yl),
        k_copy(3, B, yr),
        k_copy(4, B, yl),
        k_copy(5, A, yr),
        k_copy(6, A, y2),
        k_copy(7, B, y2),
    ]
    for i in range(4):
        gs[i].start()
    ks[0].start()
    ks[1].start()
    gs[0].wait_recv()
    gs[4].start()
    ks[2].start()
    gs[1].wait_recv()
    gs[5].start()
    ks[3].start()
    for i in range(2, 6):
        gs[i].wait_recv()
        ks[i + 2].start()
    for k in ks:
        k.wait_recv()

    def disp_dot(i, carry):
        cols = pl.ds(pl.multiple_of(i * 256, 256), 256)
        w = sgb[pl.ds(i * 4, 4)].reshape(256, 768)
        d = lax.dot_general(tok[...], w, NT, preferred_element_type=F32) * dspf[:, cols]
        ddf[:, cols] = d
        dtl[:, cols] = jnp.sum(d, axis=0, keepdims=True)
        return carry

    lax.fori_loop(0, 4, disp_dot, 0)

    def dt_copy(i):
        return remote(dtl, dtb.at[s], dt_s.at[0], dt_r.at[0], group(i))

    pltpu.make_async_copy(dtl, dtb.at[s], dt_r.at[0]).start()

    def dt_start(i, carry):
        dt_copy(i).start()
        return carry

    lax.fori_loop(1, 16, dt_start, 0)

    def direct(i, carry):
        cols = pl.ds(pl.multiple_of(i * 256, 256), 256)
        w = sgb[:, :, cols].reshape(1024, 256)
        acc[:, cols] = jnp.dot(dspb[...], w, preferred_element_type=F32)
        return carry

    lax.fori_loop(0, 3, direct, 0)
    p_g[4].wait_recv()
    pltpu.make_async_copy(dtb, dtb, dt_r.at[0]).wait()
    dots = jnp.sum(dtb[...], axis=0)

    def logit(i, carry):
        rows = pl.ds(pl.multiple_of(i * 64, 64), 64)
        cb[rows, :] = (cc[rows, :] + ddf[rows, :] - dspf[rows, :] * dots).astype(BF16)
        return carry

    lax.fori_loop(0, 8, logit, 0)

    def through(i, carry):
        cols = pl.ds(pl.multiple_of(i * 256, 256), 256)
        w = ptb[:, :, :, :, cols].reshape(1024, 256)
        t = acc[:, cols] + jnp.dot(cb[...], w, preferred_element_type=F32)
        out_ref[0, :, cols] = t.astype(BF16)
        return carry

    lax.fori_loop(0, 3, through, 0)

    for k in range(4):
        cs_copy(k).wait_send()
    for copy in ys + gs + ks + o_g + p_g + [z_o, z_p]:
        copy.wait_send()

    def drain(buf_src, sem):
        pltpu.make_async_copy(buf_src, buf_src, sem).wait()

    drain(a2r.at[pl.ds(0, 63)], a_s.at[0])
    drain(b2r.at[pl.ds(0, 63)], b_s.at[0])
    drain(stb.at[pl.ds(0, 15)], st_s.at[0])
    drain(dtb.at[pl.ds(0, 15)], dt_s.at[0])


def on_device(tokens, out_grad, saved_logits, slot_params, slot_inputs, slot_outputs, expert_in, expert_out):
    any_spec = pl.BlockSpec(memory_space=pl.ANY)
    vm = pltpu.VMEM
    dma = pltpu.SemaphoreType.DMA
    return pl.pallas_call(
        kernel,
        out_shape=jax.ShapeDtypeStruct((1, 512, 768), BF16),
        in_specs=[any_spec] * 8,
        out_specs=pl.BlockSpec(memory_space=pltpu.VMEM),
        scratch_shapes=[
            vm((512, 1024), BF16),
            vm((512, 768), BF16),
            vm((512, 768), BF16),
            vm((768, 3072), BF16),
            vm((3072, 768), BF16),
            vm((16, 4, 768), BF16),
            vm((512, 1024), F32),
            vm((512, 1024), BF16),
            vm((16, 64, 768), BF16),
            vm((16, 64, 384), BF16),
            vm((16, 64, 384), BF16),
            vm((6, 8, 16, 384), BF16),
            vm((2, 8, 16, 384), BF16),
            vm((16, 16, 384), F32),
            vm((16, 4, 4, 384), BF16),
            vm((64, 4, 384), BF16),
            vm((64, 768), F32),
            vm((64, 3072), F32),
            vm((16, 2, 4, 384), BF16),
            vm((64, 4, 384), BF16),
            vm((16, 16, 384), F32),
            vm((16, 64, 768), BF16),
            vm((4, 2, 2, 64, 768), BF16),
            vm((4, 2, 2, 64, 768), BF16),
            vm((512, 1024), F32),
            vm((512, 1024), F32),
            vm((512, 1024), F32),
            vm((512, 1024), BF16),
            vm((2, 1024), F32),
            vm((16, 2, 1024), F32),
            vm((1, 1024), F32),
            vm((16, 1, 1024), F32),
            vm((512, 768), F32),
            dma((8,)),
            dma((4,)), dma((4,)),
            dma((6,)), dma((6,)),
            dma((1,)), dma((1,)),
            dma((1,)), dma((1,)),
            dma((6,)), dma((6,)),
            dma((8,)), dma((8,)),
            dma((6,)), dma((6,)),
            dma((6,)), dma((6,)),
            dma((1,)), dma((1,)),
            dma((1,)), dma((1,)),
        ],
        compiler_params=pltpu.CompilerParams(
            collective_id=0, has_side_effects=True, vmem_limit_bytes=60 * 1024 * 1024
        ),
    )(tokens, out_grad, saved_logits, slot_params.T, slot_inputs, slot_outputs, expert_in, expert_out)


def solution(mesh):
    placed = (
        P("clip", "seq", None),
        P("clip", "seq", None),
        P("clip", "seq", None),
        P(None, "seq"),
        P(None, ("clip", "seq"), None),
        P("clip", "seq", None),
        P(("clip", "seq"), None, None),
        P(("clip", "seq"), None, None),
    )
    return jax.shard_map(
        on_device, mesh=mesh, in_specs=placed, out_specs=P("clip", "seq", None), check_vma=False
    )
```

time: 302 us -> 67 us (0.22)
  waiting for transfers between devices: 163 us -> 0 us
  blocking collectives: 77 us -> 0 us
  Pallas kernels: 0 us -> 64.8 us
  matrix products: 28.2 us -> 0 us
  between operations: 13.3 us -> 0.01 us
  starting transfers between devices: 8.51 us -> 0 us
  local copies, waits for them, and re-layouts: 7.55 us -> 2.06 us
  other arithmetic: 4.06 us -> 0 us
    psum x1 -> x0, waiting for transfers between devices: 131 us -> none  [on_device(): summed = lax.psum(partial_cot.astype(jnp.bfloat16), 'seq')]
    pallas_call x0 -> x1, Pallas kernels: none -> 64.8 us  [on_device(): pl.pallas_call(kernel, out_shape=jax.ShapeDtypeStruct((1, 512, 768), BF16...]
    all_gather x2 -> x0, blocking collectives: 37.7 us -> none  [combined_all(): pieces = jax.tree.map(lambda part: lax.all_gather(part, axis), value)]
    dot_general x7 -> x0, matrix products: 28.2 us -> none  [the longest x1 6.78 us: on_device(): jnp.einsum('cejh,edh->cejd', hidden_cot, expert_in, preferred_element_typ...]
    psum x1 -> x0, blocking collectives: 27 us -> none  [on_device(): slot_dots = lax.psum(jnp.sum(dispatch * disp_cot, axis=0), 'seq')]
    all_gather x3 -> x0, waiting for transfers between devices: 24.5 us -> none  [the longest x1 21.3 us: on_device(): lax.all_gather(slot_outputs, 'seq', axis=1, tiled=True)]
    all_to_all x1 -> x0, blocking collectives: 12.2 us -> none  [on_device(): lax.all_to_all(local_grad, 'clip', split_axis=0, concat_axis=0, tiled=True)]
    all_to_all x1 -> x0, starting transfers between devices: 8.39 us -> none  [on_device(): lax.all_to_all(mine, 'clip', split_axis=0, concat_axis=0, tiled=True)]
  transfers between devices with their start and end apart: 5 -> 0, of which waited for: 4 -> 0; matrix products, arithmetic and copies ran while one was open for 6% -> 0% of each run, Pallas kernels for 0% -> 0%
where the time goes in v1:
time: 67 us; the launch traced here: 66.8 us
  Pallas kernels  64.8 us (97%)
  local copies, waits for them, and re-layouts  2.06 us (3%)
    pallas_call x1, Pallas kernels, on_device(): pl.pallas_call(kernel, out_shape=jax.ShapeDtypeStruct((1, 512, 768), BF16...  64.8 us
    unnamed x1, local copies, waits for them, and re-layouts  2.06 us

profile of v1, /device:TPU:1, one launch (start us, length us, event | category | flops | bytes accessed | tf_op | source)
XLA Modules:
  0.0 66.8 jit_solution(13480613434778463790)
XLA Ops:
  0.0 64.8 %shard_map.82 = bf16[1,512,768]{2,1,0:T(8,128)(2,1)} custom-call(bf16[1,512,768]{2,1,0:T(8,128)(2,1)} %tok_h.1, bf16[1,512,768]{2,1,0:T(8,128)(2,1)} %og_h.1, bf16[1,512,1024]{2,1,0:T(8,128)(2,1)} %lg_h.1, bf16[64,768]{1,0:T(8,128)(2,1)} %bitcast.1, bf16[16,4,768]{2,1,0:T(4,128)(2,1)} %xin_h.1, bf16[1,64,768]{2,1,0:T(8,128)(2,1)} %so_h.1, ...), custom_call_target="tpu_custom_call" | custom-call | tf_op jit(solution)/shard_map/pallas_call | solution.py:415
  64.8 2.1 %copy.10 = bf16[1,512,768]{2,1,0:T(8,128)(2,1)} copy(bf16[1,512,768]{2,1,0:T(8,128)(2,1)} %shard_map.82) | data formatting | bytes 1572864

commit v2 on v1

--- a/solution.py
+++ b/solution.py
@@ -20,7 +20,7 @@
 
 def kernel(
     tok_h, og_h, lg_h, pt_h, xin_h, so_h, win_h, wout_h, out_ref,
-    lg, og, tok, win, wout, xin, cf, cb, pb, rp, hb, ry, st, qf, a2s, a2r, xf, gp, b2s, b2r, zf, sgb,
+    lg, og, tok, win, wout, xin, cf, cb, pb, rp, hb, ry, st, qf, a2s, a2r, xf, gp, hc, b2s, b2r, zf, sgb,
     ob, ptb, cc, ddf, dspf, dspb, stl, stb, dtl, dtb, acc,
     ld, cs_s, cs_r, y_s, y_r, a_s, a_r, b_s, b_r, g_s, g_r, k_s, k_r, o_s, o_r, p_s, p_r, st_s, st_r, dt_s, dt_r,
 ):
@@ -43,8 +43,18 @@
             src_ref=src, dst_ref=dst, send_sem=ssem, recv_sem=rsem, device_id=dev, device_id_type=MESH
         )
 
-    def plane(i):
-        return ((c + i // 4) % 16, y * 4 + (q + i % 4) % 4)
+    def far(k):
+        return ((c // 4 + 3 - k // 4) % 4) * 4 + (c + 3 - k % 4) % 4
+
+    def to_plane(send):
+        def step(k, carry):
+            for t in range(4):
+                send(far(k), t)
+            return carry
+
+        lax.fori_loop(0, 15, step, 0)
+        for t in range(1, 4):
+            send(c, (q + t) % 4)
 
     def group(i):
         return (c, (s + i) % 16)
@@ -64,9 +74,8 @@
 
     barrier = pltpu.get_barrier_semaphore()
 
-    def greet_plane(i, carry):
-        pl.semaphore_signal(barrier, inc=1, device_id=plane(i), device_id_type=MESH)
-        return carry
+    def greet_plane(cd, t):
+        pl.semaphore_signal(barrier, inc=1, device_id=(cd, y * 4 + t), device_id_type=MESH)
 
     def greet_group(i, carry):
         pl.semaphore_signal(
@@ -74,8 +83,8 @@
         )
         return carry
 
+    to_plane(greet_plane)
     lax.fori_loop(0, 12, greet_group, 0)
-    lax.fori_loop(1, 64, greet_plane, 0)
 
     loads[0].wait()
 
@@ -88,9 +97,8 @@
         cb[rows, :] = comb.astype(BF16)
         return carry
 
-    lax.fori_loop(0, 8, front, 0)
+    lax.fori_loop(0, 8, front, 0, unroll=2)
     loads[1].wait()
-    pl.semaphore_wait(barrier, 75)
 
     def cs_copy(k):
         part = pl.ds(k * 4, 4)
@@ -100,10 +108,14 @@
         cols = pl.ds(pl.multiple_of(k * 256, 256), 256)
         p = lax.dot_general(cb[:, cols], og[...], TN, preferred_element_type=F32)
         pb[pl.ds(k * 4, 4)] = p.astype(BF16).reshape(4, 64, 768)
+        return carry
+
+    lax.fori_loop(0, 3, partial, 0)
+    pl.semaphore_wait(barrier, 75)
+    for k in range(3):
         cs_copy(k).start()
-        return carry
-
-    lax.fori_loop(0, 4, partial, 0)
+    partial(3, 0)
+    cs_copy(3).start()
 
     loads[2].wait()
     loads[3].wait()
@@ -133,8 +145,8 @@
         y_copy(4, st.at[0], right),
         y_copy(5, st.at[1], left),
     ]
-    for i in range(4):
-        ys[i].start()
+    ys[0].start()
+    ys[1].start()
 
     loads[4].wait()
     loads[5].wait()
@@ -143,12 +155,17 @@
     xin_b = xf[...].astype(BF16)
 
     def slope(i, carry):
-        cols = pl.ds(pl.multiple_of(i * 512, 512), 512)
-        hid = jnp.dot(xin_b, win[:, cols], preferred_element_type=F32)
-        gp[:, cols] = gelu_slope(hid)
-        return carry
-
-    lax.fori_loop(0, 6, slope, 0)
+        part = pl.ds(pl.multiple_of(i * 512, 512), 512)
+        hid = jnp.dot(xin_b, win[:, part], preferred_element_type=F32)
+        gp[:, part] = gelu_slope(hid)
+        return carry
+
+    lax.fori_loop(0, 3, slope, 0)
+    ys[0].wait_send()
+    ys[1].wait_send()
+    ys[2].start()
+    ys[3].start()
+    lax.fori_loop(3, 6, slope, 0)
 
     ys[0].wait_recv()
     st[0] = (ry[0].astype(F32) + hb[A, rows_of(yr), :].astype(F32)).astype(BF16)
@@ -168,36 +185,37 @@
 
     o_g = gather(ob, o_s, o_r)
     p_g = gather(ptb, p_s, p_r)
+    def colmax(i, m):
+        rows = pl.ds(pl.multiple_of(i * 64, 64), 64)
+        return jnp.maximum(m, jnp.max(lg[rows, :].astype(F32), axis=0, keepdims=True))
+
+    m_loc = lax.fori_loop(1, 8, colmax, jnp.max(lg[0:64, :].astype(F32), axis=0, keepdims=True))
+
+    def colsum(i, t):
+        rows = pl.ds(pl.multiple_of(i * 64, 64), 64)
+        return t + jnp.sum(jnp.exp(lg[rows, :].astype(F32) - m_loc), axis=0, keepdims=True)
+
+    s_loc = lax.fori_loop(0, 8, colsum, jnp.zeros((1, 1024), F32))
+    stl[0:1, :] = m_loc
+    stl[1:2, :] = s_loc
+
+    def st_copy(i):
+        return remote(stl, stb.at[s], st_s.at[0], st_r.at[0], group(i))
+
+    own_st = pltpu.make_async_copy(stl, stb.at[s], st_r.at[0])
+    own_st.start()
+
+    def st_start(i, carry):
+        st_copy(i).start()
+        return carry
+
+    lax.fori_loop(1, 16, st_start, 0)
+
+    ys[4].wait_send()
+    ys[5].wait_send()
     z_o.wait_recv()
     o_g[0].start()
     o_g[1].start()
-
-    def colmax(i, m):
-        rows = pl.ds(pl.multiple_of(i * 64, 64), 64)
-        return jnp.maximum(m, jnp.max(lg[rows, :].astype(F32), axis=0, keepdims=True))
-
-    m_loc = lax.fori_loop(1, 8, colmax, jnp.max(lg[0:64, :].astype(F32), axis=0, keepdims=True))
-
-    def colsum(i, t):
-        rows = pl.ds(pl.multiple_of(i * 64, 64), 64)
-        return t + jnp.sum(jnp.exp(lg[rows, :].astype(F32) - m_loc), axis=0, keepdims=True)
-
-    s_loc = lax.fori_loop(0, 8, colsum, jnp.zeros((1, 1024), F32))
-    stl[0:1, :] = m_loc
-    stl[1:2, :] = s_loc
-
-    def st_copy(i):
-        return remote(stl, stb.at[s], st_s.at[0], st_r.at[0], group(i))
-
-    own_st = pltpu.make_async_copy(stl, stb.at[s], st_r.at[0])
-    own_st.start()
-
-    def st_start(i, carry):
-        st_copy(i).start()
-        return carry
-
-    lax.fori_loop(1, 16, st_start, 0)
-
     ys[3].wait_recv()
     ys[4].wait_recv()
     qf[0:8] = hb[A, rows_of(y), :].astype(F32) + ry[3].astype(F32) + ry[4].astype(F32)
@@ -207,13 +225,11 @@
     for i in range(4):
         a2s[:, i] = qf[:, 4 * i : 4 * i + 4, :].astype(BF16)
 
-    def a_start(i, carry):
-        cd, sd = plane(i)
-        remote(a2s.at[cd, sd % 4], a2r.at[c * 4 + q], a_s.at[0], a_r.at[0], (cd, sd)).start()
-        return carry
+    def a_start(cd, t):
+        remote(a2s.at[cd, t], a2r.at[c * 4 + q], a_s.at[0], a_r.at[0], (cd, y * 4 + t)).start()
 
     pltpu.make_async_copy(a2s.at[c, q], a2r.at[c * 4 + q], a_r.at[0]).start()
-    lax.fori_loop(1, 64, a_start, 0)
+    to_plane(a_start)
 
     z_p.wait_recv()
     p_g[0].start()
@@ -246,27 +262,30 @@
                 a2r[4 * i + j].astype(F32) + a2r[4 * i + 2 + j].astype(F32)
             )
     x_b = xf[...].astype(BF16)
-    xf[...] = jnp.zeros((64, 768), F32)
-
-    def expert(i, carry):
-        part = pl.ds(pl.multiple_of(i * 512, 512), 512)
-        act = lax.dot_general(x_b, wout[part, :], NT, preferred_element_type=F32)
-        hc = (act * gp[:, part]).astype(BF16)
-        xf[...] += lax.dot_general(hc, win[:, part], NT, preferred_element_type=F32)
-        return carry
-
-    lax.fori_loop(0, 6, expert, 0)
+
+    def act(i, carry):
+        part = pl.ds(pl.multiple_of(i * 1024, 1024), 1024)
+        a = lax.dot_general(x_b, wout[part, :], NT, preferred_element_type=F32)
+        hc[:, part] = (a * gp[:, part]).astype(BF16)
+        return carry
+
+    lax.fori_loop(0, 3, act, 0)
+
+    def grad(i, carry):
+        part = pl.ds(pl.multiple_of(i * 256, 256), 256)
+        xf[:, part] = lax.dot_general(hc[...], win[part, :], NT, preferred_element_type=F32)
+        return carry
+
+    lax.fori_loop(0, 3, grad, 0)
     for i in range(16):
         for j in range(2):
             b2s[i, j] = xf[4 * i : 4 * i + 4, 384 * j : 384 * j + 384].astype(BF16)
 
-    def b_start(i, carry):
-        cd, sd = plane(i)
-        remote(b2s.at[cd, sd % 2], b2r.at[c * 4 + q], b_s.at[0], b_r.at[0], (cd, sd)).start()
-        return carry
+    def b_start(cd, t):
+        remote(b2s.at[cd, t % 2], b2r.at[c * 4 + q], b_s.at[0], b_r.at[0], (cd, y * 4 + t)).start()
 
     pltpu.make_async_copy(b2s.at[c, h], b2r.at[c * 4 + q], b_r.at[0]).start()
-    lax.fori_loop(1, 64, b_start, 0)
+    to_plane(b_start)
 
     o_g[2].wait_recv()
     o_g[3].wait_recv()
@@ -330,10 +349,14 @@
         k_copy(6, A, y2),
         k_copy(7, B, y2),
     ]
-    for i in range(4):
-        gs[i].start()
+    gs[0].start()
+    gs[1].start()
     ks[0].start()
     ks[1].start()
+    gs[0].wait_send()
+    gs[1].wait_send()
+    gs[2].start()
+    gs[3].start()
     gs[0].wait_recv()
     gs[4].start()
     ks[2].start()
@@ -396,7 +419,7 @@
 
     for k in range(4):
         cs_copy(k).wait_send()
-    for copy in ys + gs + ks + o_g + p_g + [z_o, z_p]:
+    for copy in ys[2:4] + gs[2:] + ks + o_g + p_g + [z_o, z_p]:
         copy.wait_send()
 
     def drain(buf_src, sem):
@@ -414,7 +437,7 @@
     dma = pltpu.SemaphoreType.DMA
     return pl.pallas_call(
         kernel,
-        out_shape=jax.ShapeDtypeStruct((1, 512, 768), BF16),
+        out_shape=pltpu.VMEM((1, 512, 768), BF16),
         in_specs=[any_spec] * 8,
         out_specs=pl.BlockSpec(memory_space=pltpu.VMEM),
         scratch_shapes=[
@@ -436,6 +459,7 @@
             vm((64, 4, 384), BF16),
             vm((64, 768), F32),
             vm((64, 3072), F32),
+            vm((64, 3072), BF16),
             vm((16, 2, 4, 384), BF16),
             vm((64, 4, 384), BF16),
             vm((16, 16, 384), F32),

time: 67 us -> 62.3 us (0.930)
  Pallas kernels: 64.8 us -> 61.4 us
  local copies, waits for them, and re-layouts: 2.06 us -> 0.88 us
    pallas_call x1, Pallas kernels: 64.8 us -> 61.4 us  [on_device(): pl.pallas_call(kernel, out_shape=pltpu.VMEM((1, 512, 768), BF16), in_spec...]
    unnamed x1, local copies, waits for them, and re-layouts: 2.06 us -> 0.88 us
where the time goes in v2:
time: 62.3 us; the launch traced here: 62.2 us
  Pallas kernels  61.4 us (99%)
  local copies, waits for them, and re-layouts  0.88 us (1%)
    pallas_call x1, Pallas kernels, on_device(): pl.pallas_call(kernel, out_shape=pltpu.VMEM((1, 512, 768), BF16), in_spec...  61.4 us

profile of v2, /device:TPU:1, one launch (start us, length us, event | category | flops | bytes accessed | tf_op | source)
XLA Modules:
  0.0 62.2 jit_solution(7962991064329238842)
XLA Ops:
  0.0 61.4 %shard_map.82 = bf16[1,512,768]{2,1,0:T(8,128)(2,1)S(1)} custom-call(bf16[1,512,768]{2,1,0:T(8,128)(2,1)} %tok_h.1, bf16[1,512,768]{2,1,0:T(8,128)(2,1)} %og_h.1, bf16[1,512,1024]{2,1,0:T(8,128)(2,1)} %lg_h.1, bf16[64,768]{1,0:T(8,128)(2,1)} %bitcast.1, bf16[16,4,768]{2,1,0:T(4,128)(2,1)} %xin_h.1, bf16[1,64,768]{2,1,0:T(8,128)(2,1)} %so_h.1, ...), custom_call_target="tpu_custom_call" | custom-call | tf_op jit(solution)/shard_map/pallas_call | solution.py:438
  61.4 0.9 %copy.10 = bf16[1,512,768]{2,1,0:T(8,128)(2,1)} copy(bf16[1,512,768]{2,1,0:T(8,128)(2,1)S(1)} %shard_map.82) | data formatting | bytes 1572864

commit v3 on v2

--- a/solution.py
+++ b/solution.py
@@ -20,14 +20,17 @@
 
 def kernel(
     tok_h, og_h, lg_h, pt_h, xin_h, so_h, win_h, wout_h, out_ref,
-    lg, og, tok, win, wout, xin, cf, cb, pb, rp, hb, ry, st, qf, a2s, a2r, xf, gp, hc, b2s, b2r, zf, sgb,
-    ob, ptb, cc, ddf, dspf, dspb, stl, stb, dtl, dtb, acc,
-    ld, cs_s, cs_r, y_s, y_r, a_s, a_r, b_s, b_r, g_s, g_r, k_s, k_r, o_s, o_r, p_s, p_r, st_s, st_r, dt_s, dt_r,
+    lg, og, tok, win, wout, xin, cf, cb, pb, rp, hb, ry, st, qf, a2s, a2r, xf, gp, hc, b2s, b2r, zf, sp,
+    ob, cc, dspf, lw, stl, s1b, s1l, s2b, dtl, dtb, acc, lgp, xp, xrp, hx, xry, xst, xq,
+    ld, cs_s, cs_r, y_s, y_r, a_s, a_r, b_s, b_r, g_s, g_r, k_s, k_r, o_s, o_r, p_s, p_r, s1_s, s1_r, s2_s, s2_r, dt_s, dt_r, xc_s, xc_r, x_s, x_r,
 ):
+    sgb, ptx = sp.at[0], sp.at[1].reshape(4, 2, 2, 4, 16, 768)
     c = lax.axis_index("clip")
     s = lax.axis_index("seq")
     y, q, h = s // 4, s % 4, s % 2
     zl = q // 2
+    x, zh = c // 4, c % 4
+    xr, xl = (x + 1) % 4, (x + 3) % 4
     yr, y2, yl = (y + 1) % 4, (y + 2) % 4, (y + 3) % 4
     right, left = (c, yr * 4 + q), (c, yl * 4 + q)
     mate = (c, s + 1 - 2 * h)
@@ -63,7 +66,7 @@
         pltpu.make_async_copy(lg_h.at[0], lg, ld.at[0]),
         pltpu.make_async_copy(og_h.at[0], og, ld.at[1]),
         pltpu.make_async_copy(so_h.at[0], ob.at[y, zl, h], ld.at[2]),
-        pltpu.make_async_copy(pt_h, ptb.at[y, zl, h], ld.at[3]),
+        pltpu.make_async_copy(pt_h.at[rows_of(x)], ptx.at[y, zl, h, x], ld.at[3]),
         pltpu.make_async_copy(xin_h, xin, ld.at[4]),
         pltpu.make_async_copy(win_h.at[0], win, ld.at[5]),
         pltpu.make_async_copy(wout_h.at[0], wout, ld.at[6]),
@@ -100,9 +103,9 @@
     lax.fori_loop(0, 8, front, 0, unroll=2)
     loads[1].wait()
 
-    def cs_copy(k):
-        part = pl.ds(k * 4, 4)
-        return remote(pb.at[part, :, other], rp.at[part], cs_s.at[k], cs_r.at[k], mate)
+    def cs_copy(i):
+        part = rows_of((y + 2 + i) % 4)
+        return remote(pb.at[:, part, other], rp.at[:, part], cs_s.at[0], cs_r.at[i], mate)
 
     def partial(k, carry):
         cols = pl.ds(pl.multiple_of(k * 256, 256), 256)
@@ -110,27 +113,37 @@
         pb[pl.ds(k * 4, 4)] = p.astype(BF16).reshape(4, 64, 768)
         return carry
 
-    lax.fori_loop(0, 3, partial, 0)
+    lax.fori_loop(0, 4, partial, 0)
     pl.semaphore_wait(barrier, 75)
-    for k in range(3):
-        cs_copy(k).start()
-    partial(3, 0)
-    cs_copy(3).start()
-
+    for i in range(4):
+        cs_copy(i).start()
+
+    def p_copy(i, ref, dev):
+        return remote(ref, ref, p_s.at[i], p_r.at[i], dev)
+
+    x_right, x_left = (xr * 4 + zh, s), (xl * 4 + zh, s)
+    ps = [
+        p_copy(0, ptx.at[y, zl, h, x], right),
+        p_copy(1, ptx.at[y, zl, h, x], left),
+        p_copy(2, ptx.at[y, zl, h, x], (c, y2 * 4 + q)),
+        p_copy(3, ptx.at[:, zl, h, x], zmate),
+        p_copy(4, ptx.at[:, :, h, x], x_right),
+        p_copy(5, ptx.at[:, :, h, x], x_left),
+        p_copy(6, ptx.at[:, 0, h, xl], x_right),
+        p_copy(7, ptx.at[:, 1, h, xr], x_left),
+        p_copy(8, ptx.at[:, :, h], mate),
+    ]
     loads[2].wait()
     loads[3].wait()
     z_o = remote(ob.at[y, zl, h], ob.at[y, zl, h], o_s.at[0], o_r.at[0], zmate)
-    z_p = remote(ptb.at[y, zl, h], ptb.at[y, zl, h], p_s.at[0], p_r.at[0], zmate)
     z_o.start()
-    z_p.start()
-
-    def half_sum(k, carry):
-        part = pl.ds(k * 4, 4)
-        cs_copy(k).wait_recv()
-        hb[part] = (pb[part, :, mine].astype(F32) + rp[part].astype(F32)).astype(BF16)
-        return carry
-
-    lax.fori_loop(0, 4, half_sum, 0)
+    for i in range(3):
+        ps[i].start()
+
+    def half_sum(i):
+        part = rows_of((y + 2 + i) % 4)
+        cs_copy(i).wait_recv()
+        hb[:, part, :] = (pb[:, part, mine].astype(F32) + rp[:, part, :].astype(F32)).astype(BF16)
 
     A, B = pl.ds(0, 8), pl.ds(8, 8)
 
@@ -145,27 +158,54 @@
         y_copy(4, st.at[0], right),
         y_copy(5, st.at[1], left),
     ]
+    half_sum(0)
     ys[0].start()
     ys[1].start()
-
-    loads[4].wait()
-    loads[5].wait()
-    for i in range(16):
-        xf[4 * i : 4 * i + 4, :] = xin[i].astype(F32)
-    xin_b = xf[...].astype(BF16)
-
-    def slope(i, carry):
-        part = pl.ds(pl.multiple_of(i * 512, 512), 512)
-        hid = jnp.dot(xin_b, win[:, part], preferred_element_type=F32)
-        gp[:, part] = gelu_slope(hid)
-        return carry
-
-    lax.fori_loop(0, 3, slope, 0)
+    for i in range(1, 4):
+        half_sum(i)
+
+    def reorder(k, carry):
+        p = lax.broadcasted_iota(jnp.int32, (1, 256), 1)
+        pick = lax.broadcasted_iota(jnp.int32, (1024, 256), 0) == (p // 16) * 64 + p % 16 + k * 16
+        part = jnp.dot(lg[...], pick.astype(F32).astype(BF16), preferred_element_type=F32)
+        lgp[k] = part.astype(BF16)
+        return carry
+
+    lax.fori_loop(0, 2, reorder, 0)
     ys[0].wait_send()
     ys[1].wait_send()
     ys[2].start()
     ys[3].start()
-    lax.fori_loop(3, 6, slope, 0)
+    for i in range(3):
+        ps[i].wait_recv()
+    ps[3].start()
+    lax.fori_loop(2, 4, reorder, 0)
+
+    def stats(k, carry):
+        part = lgp[k].astype(F32)
+        top_k = jnp.max(part, axis=0, keepdims=True)
+        stl[k, 0:1, :] = top_k
+        stl[k, 1:2, :] = jnp.sum(jnp.exp(part - top_k), axis=0, keepdims=True)
+        return carry
+
+    lax.fori_loop(0, 4, stats, 0)
+
+    def merged(buf):
+        top = jnp.max(buf[:, 0, :], axis=0, keepdims=True)
+        return top, jnp.sum(buf[:, 1, :] * jnp.exp(buf[:, 0, :] - top), axis=0, keepdims=True)
+
+    def others(t):
+        return y * 4 + (q + t) % 4
+
+    s1 = [remote(stl.at[(q + t) % 4], s1b.at[q], s1_s.at[0], s1_r.at[0], (c, others(t))) for t in range(1, 4)]
+
+    def s2_start(i, carry):
+        remote(s1l, s2b.at[q, y], s2_s.at[0], s2_r.at[0], group(i)).start()
+        return carry
+
+    pltpu.make_async_copy(stl.at[q], s1b.at[q], s1_r.at[0]).start()
+    for copy in s1:
+        copy.start()
 
     ys[0].wait_recv()
     st[0] = (ry[0].astype(F32) + hb[A, rows_of(yr), :].astype(F32)).astype(BF16)
@@ -184,32 +224,27 @@
         ]
 
     o_g = gather(ob, o_s, o_r)
-    p_g = gather(ptb, p_s, p_r)
-    def colmax(i, m):
-        rows = pl.ds(pl.multiple_of(i * 64, 64), 64)
-        return jnp.maximum(m, jnp.max(lg[rows, :].astype(F32), axis=0, keepdims=True))
-
-    m_loc = lax.fori_loop(1, 8, colmax, jnp.max(lg[0:64, :].astype(F32), axis=0, keepdims=True))
-
-    def colsum(i, t):
-        rows = pl.ds(pl.multiple_of(i * 64, 64), 64)
-        return t + jnp.sum(jnp.exp(lg[rows, :].astype(F32) - m_loc), axis=0, keepdims=True)
-
-    s_loc = lax.fori_loop(0, 8, colsum, jnp.zeros((1, 1024), F32))
-    stl[0:1, :] = m_loc
-    stl[1:2, :] = s_loc
-
-    def st_copy(i):
-        return remote(stl, stb.at[s], st_s.at[0], st_r.at[0], group(i))
-
-    own_st = pltpu.make_async_copy(stl, stb.at[s], st_r.at[0])
-    own_st.start()
-
-    def st_start(i, carry):
-        st_copy(i).start()
-        return carry
-
-    lax.fori_loop(1, 16, st_start, 0)
+    loads[4].wait()
+    loads[5].wait()
+    for i in range(16):
+        xf[4 * i : 4 * i + 4, :] = xin[i].astype(F32)
+    xin_b = xf[...].astype(BF16)
+
+    def slope(i, carry):
+        part = pl.ds(pl.multiple_of(i * 512, 512), 512)
+        hid = jnp.dot(xin_b, win[:, part], preferred_element_type=F32)
+        gp[:, part] = gelu_slope(hid)
+        return carry
+
+    lax.fori_loop(0, 3, slope, 0)
+    pltpu.make_async_copy(s1b, s1b, s1_r.at[0]).wait()
+    ps[3].wait_recv()
+    ps[4].start()
+    ps[5].start()
+    s1l[0:1, :], s1l[1:2, :] = merged(s1b)
+    pltpu.make_async_copy(s1l, s2b.at[q, y], s2_r.at[0]).start()
+    lax.fori_loop(1, 16, s2_start, 0)
+    lax.fori_loop(3, 6, slope, 0)
 
     ys[4].wait_send()
     ys[5].wait_send()
@@ -231,28 +266,55 @@
     pltpu.make_async_copy(a2s.at[c, q], a2r.at[c * 4 + q], a_r.at[0]).start()
     to_plane(a_start)
 
-    z_p.wait_recv()
-    p_g[0].start()
-    p_g[1].start()
+    loads[7].wait()
+    pltpu.make_async_copy(s2b, s2b, s2_r.at[0]).wait()
+
+    def xc_copy(i, k):
+        return remote(xp.at[k, :, other], xrp.at[k], xc_s.at[0], xc_r.at[i], mate)
+
+    def disp(i, carry):
+        k = (y + 2 + i) % 4
+        top, total = merged(s2b.at[k])
+        d = jnp.exp(lgp[k].astype(F32) - top) * (1.0 / total)
+        dspf[k] = d
+        lw[k, :, 0:256] = d.astype(BF16)
+        xp[k] = lax.dot_general(lw[k, :, 0:256], tok[...], TN, preferred_element_type=F32).astype(BF16)
+        xc_copy(i, k).start()
+        return carry
+
+    lax.fori_loop(0, 4, disp, 0)
+
     o_g[0].wait_recv()
     o_g[2].start()
     o_g[1].wait_recv()
     o_g[3].start()
 
-    pltpu.make_async_copy(stb, stb, st_r.at[0]).wait()
-    m_all = stb[:, 0, :]
-    top = jnp.max(m_all, axis=0, keepdims=True)
-    total = jnp.sum(stb[:, 1, :] * jnp.exp(m_all - top), axis=0, keepdims=True)
-    inv_total = 1.0 / total
-
-    def disp(i, carry):
-        rows = pl.ds(pl.multiple_of(i * 64, 64), 64)
-        d = jnp.exp(lg[rows, :].astype(F32) - top) * inv_total
-        dspf[rows, :] = d
-        dspb[rows, :] = d.astype(BF16)
-        return carry
-
-    lax.fori_loop(0, 8, disp, 0)
+    def x_half(i, carry):
+        k = (y + 2 + i) % 4
+        xc_copy(i, k).wait_recv()
+        hx[k] = (xp[k, :, mine].astype(F32) + xrp[k].astype(F32)).astype(BF16)
+        return carry
+
+    lax.fori_loop(0, 4, x_half, 0)
+    XA, XB = pl.ds(0, 128), pl.ds(128, 128)
+
+    def x_copy(i, src, dev):
+        return remote(src, xry.at[i], x_s.at[0], x_r.at[i], dev)
+
+    xs = [
+        x_copy(0, hx.at[y2, XA], right),
+        x_copy(1, hx.at[y2, XB], left),
+        x_copy(2, hx.at[yr, XB], right),
+        x_copy(3, hx.at[yl, XA], left),
+        x_copy(4, xst.at[0], right),
+        x_copy(5, xst.at[1], left),
+    ]
+    xs[0].start()
+    xs[1].start()
+    ps[4].wait_recv()
+    ps[6].start()
+    ps[5].wait_recv()
+    ps[7].start()
 
     loads[6].wait()
     pltpu.make_async_copy(a2r, a2r, a_r.at[0]).wait()
@@ -270,6 +332,11 @@
         return carry
 
     lax.fori_loop(0, 3, act, 0)
+    xs[2].start()
+    xs[3].start()
+    o_g[2].wait_recv()
+    o_g[3].wait_recv()
+    o_g[4].start()
 
     def grad(i, carry):
         part = pl.ds(pl.multiple_of(i * 256, 256), 256)
@@ -287,13 +354,15 @@
     pltpu.make_async_copy(b2s.at[c, h], b2r.at[c * 4 + q], b_r.at[0]).start()
     to_plane(b_start)
 
-    o_g[2].wait_recv()
-    o_g[3].wait_recv()
-    o_g[4].start()
-    p_g[0].wait_recv()
-    p_g[2].start()
-    p_g[1].wait_recv()
-    p_g[3].start()
+    xs[0].wait_recv()
+    xst[0] = (xry[0].astype(F32) + hx[yr, XA, :].astype(F32)).astype(BF16)
+    xs[4].start()
+    xs[1].wait_recv()
+    xst[1] = (xry[1].astype(F32) + hx[yl, XB, :].astype(F32)).astype(BF16)
+    xs[5].start()
+    ps[6].wait_recv()
+    ps[7].wait_recv()
+    ps[8].start()
     o_g[4].wait_recv()
 
     def comb_dot(i, carry):
@@ -308,15 +377,24 @@
         rows = pl.ds(pl.multiple_of(i * 64, 64), 64)
         comb = cf[rows, :]
         v = cc[rows, :]
-        cc[rows, :] = comb * (v - jnp.sum(comb * v, axis=1, keepdims=True))
+        cb[rows, :] = (comb * (v - jnp.sum(comb * v, axis=1, keepdims=True))).astype(BF16)
         return carry
 
     lax.fori_loop(0, 8, comb_grad, 0)
-    p_g[2].wait_recv()
-    p_g[3].wait_recv()
-    p_g[4].start()
-
-    loads[7].wait()
+    ps[8].wait_recv()
+
+    def comb_out(i, carry):
+        cols = pl.ds(pl.multiple_of(i * 256, 256), 256)
+        w = sp[1, :, :, cols].reshape(1024, 256)
+        acc[:, cols] = jnp.dot(cb[...], w, preferred_element_type=F32)
+        return carry
+
+    lax.fori_loop(0, 3, comb_out, 0)
+    for i in range(2, 6):
+        xs[i].wait_recv()
+    xq[XA, :] = hx[y, XA, :].astype(F32) + xry[3].astype(F32) + xry[4].astype(F32)
+    xq[XB, :] = hx[y, XB, :].astype(F32) + xry[2].astype(F32) + xry[5].astype(F32)
+
     pltpu.make_async_copy(b2r, b2r, b_r.at[0]).wait()
     back = b2r[...].reshape(16, 4, 4, 384)
     for i in range(4):
@@ -325,11 +403,11 @@
 
     def g_copy(i, part, yy, dev):
         ref = sgb.at[part, rows_of(yy), mine]
-        return remote(ref, ref, g_s.at[i], g_r.at[i], dev)
+        return remote(ref, ref, g_s.at[min(i, 2)], g_r.at[i], dev)
 
     def k_copy(i, part, yy):
         ref = sgb.at[part, rows_of(yy), mine]
-        return remote(ref, ref, k_s.at[i], k_r.at[i], mate)
+        return remote(ref, ref, k_s.at[0], k_r.at[i], mate)
 
     gs = [
         g_copy(0, A, y, right),
@@ -353,6 +431,22 @@
     gs[1].start()
     ks[0].start()
     ks[1].start()
+
+    prod = zf[...].reshape(256, 384) * xq[...]
+    ones = jnp.ones((8, 384), F32)
+    dots = lax.dot_general(ones, prod, NT, precision=lax.Precision.HIGHEST, preferred_element_type=F32)
+    dtl[...] = dots[0:1, :]
+
+    def dt_copy(i):
+        return remote(dtl, dtb.at[s], dt_s.at[0], dt_r.at[0], group(i))
+
+    pltpu.make_async_copy(dtl, dtb.at[s], dt_r.at[0]).start()
+
+    def dt_start(i, carry):
+        dt_copy(i).start()
+        return carry
+
+    lax.fori_loop(1, 16, dt_start, 0)
     gs[0].wait_send()
     gs[1].wait_send()
     gs[2].start()
@@ -363,71 +457,54 @@
     gs[1].wait_recv()
     gs[5].start()
     ks[3].start()
-    for i in range(2, 6):
-        gs[i].wait_recv()
-        ks[i + 2].start()
-    for k in ks:
-        k.wait_recv()
-
-    def disp_dot(i, carry):
-        cols = pl.ds(pl.multiple_of(i * 256, 256), 256)
-        w = sgb[pl.ds(i * 4, 4)].reshape(256, 768)
-        d = lax.dot_general(tok[...], w, NT, preferred_element_type=F32) * dspf[:, cols]
-        ddf[:, cols] = d
-        dtl[:, cols] = jnp.sum(d, axis=0, keepdims=True)
-        return carry
-
-    lax.fori_loop(0, 4, disp_dot, 0)
-
-    def dt_copy(i):
-        return remote(dtl, dtb.at[s], dt_s.at[0], dt_r.at[0], group(i))
-
-    pltpu.make_async_copy(dtl, dtb.at[s], dt_r.at[0]).start()
-
-    def dt_start(i, carry):
-        dt_copy(i).start()
-        return carry
-
-    lax.fori_loop(1, 16, dt_start, 0)
-
-    def direct(i, carry):
-        cols = pl.ds(pl.multiple_of(i * 256, 256), 256)
-        w = sgb[:, :, cols].reshape(1024, 256)
-        acc[:, cols] = jnp.dot(dspb[...], w, preferred_element_type=F32)
-        return carry
-
-    lax.fori_loop(0, 3, direct, 0)
-    p_g[4].wait_recv()
     pltpu.make_async_copy(dtb, dtb, dt_r.at[0]).wait()
-    dots = jnp.sum(dtb[...], axis=0)
-
-    def logit(i, carry):
-        rows = pl.ds(pl.multiple_of(i * 64, 64), 64)
-        cb[rows, :] = (cc[rows, :] + ddf[rows, :] - dspf[rows, :] * dots).astype(BF16)
-        return carry
-
-    lax.fori_loop(0, 8, logit, 0)
-
-    def through(i, carry):
-        cols = pl.ds(pl.multiple_of(i * 256, 256), 256)
-        w = ptb[:, :, :, :, cols].reshape(1024, 256)
-        t = acc[:, cols] + jnp.dot(cb[...], w, preferred_element_type=F32)
-        out_ref[0, :, cols] = t.astype(BF16)
-        return carry
-
-    lax.fori_loop(0, 3, through, 0)
-
-    for k in range(4):
-        cs_copy(k).wait_send()
-    for copy in ys[2:4] + gs[2:] + ks + o_g + p_g + [z_o, z_p]:
+
+    def use(yy):
+        w = sgb[:, rows_of(yy), :].reshape(256, 768)
+        d = lax.dot_general(tok[...], w, NT, preferred_element_type=F32)
+        lw[yy, :, 256:512] = (dspf[yy] * (d - jnp.sum(dtb[pl.ds(yy * 4, 4)], axis=0))).astype(BF16)
+        both = sp[:, :, rows_of(yy), :].reshape(512, 768)
+        return jnp.dot(lw[yy], both, preferred_element_type=F32)
+
+    def add(yy):
+        acc[...] += use(yy)
+
+    ks[0].wait_recv()
+    ks[1].wait_recv()
+    add(y)
+    gs[2].wait_recv()
+    ks[4].start()
+    gs[3].wait_recv()
+    ks[5].start()
+    ks[2].wait_recv()
+    ks[4].wait_recv()
+    add(yl)
+    gs[4].wait_recv()
+    ks[6].start()
+    gs[5].wait_recv()
+    ks[7].start()
+    ks[3].wait_recv()
+    ks[5].wait_recv()
+    add(yr)
+    ks[6].wait_recv()
+    ks[7].wait_recv()
+    out_ref[0] = (acc[...] + use(y2)).astype(BF16)
+
+    for copy in ys[2:4] + o_g + ps + [z_o]:
         copy.wait_send()
 
     def drain(buf_src, sem):
         pltpu.make_async_copy(buf_src, buf_src, sem).wait()
 
+    drain(rp, cs_s.at[0])
+    drain(rp, xc_s.at[0])
+    drain(rp, k_s.at[0])
+    drain(rp.at[pl.ds(0, 12)], x_s.at[0])
+    drain(rp.at[pl.ds(0, 8)], g_s.at[2])
     drain(a2r.at[pl.ds(0, 63)], a_s.at[0])
     drain(b2r.at[pl.ds(0, 63)], b_s.at[0])
-    drain(stb.at[pl.ds(0, 15)], st_s.at[0])
+    drain(s1b.at[pl.ds(0, 3)], s1_s.at[0])
+    drain(s2b.reshape(16, 2, 256).at[pl.ds(0, 15)], s2_s.at[0])
     drain(dtb.at[pl.ds(0, 15)], dt_s.at[0])
 
 
@@ -463,29 +540,39 @@
             vm((16, 2, 4, 384), BF16),
             vm((64, 4, 384), BF16),
             vm((16, 16, 384), F32),
-            vm((16, 64, 768), BF16),
-            vm((4, 2, 2, 64, 768), BF16),
+            vm((2, 16, 64, 768), BF16),
             vm((4, 2, 2, 64, 768), BF16),
             vm((512, 1024), F32),
-            vm((512, 1024), F32),
-            vm((512, 1024), F32),
-            vm((512, 1024), BF16),
-            vm((2, 1024), F32),
-            vm((16, 2, 1024), F32),
-            vm((1, 1024), F32),
-            vm((16, 1, 1024), F32),
+            vm((4, 512, 256), F32),
+            vm((4, 512, 512), BF16),
+            vm((4, 2, 256), F32),
+            vm((4, 2, 256), F32),
+            vm((2, 256), F32),
+            vm((4, 4, 2, 256), F32),
+            vm((1, 256), F32),
+            vm((16, 1, 256), F32),
             vm((512, 768), F32),
+            vm((4, 512, 256), BF16),
+            vm((4, 256, 768), BF16),
+            vm((4, 256, 384), BF16),
+            vm((4, 256, 384), BF16),
+            vm((6, 128, 384), BF16),
+            vm((2, 128, 384), BF16),
+            vm((256, 384), F32),
             dma((8,)),
-            dma((4,)), dma((4,)),
+            dma((1,)), dma((4,)),
             dma((6,)), dma((6,)),
             dma((1,)), dma((1,)),
             dma((1,)), dma((1,)),
+            dma((3,)), dma((6,)),
+            dma((1,)), dma((8,)),
             dma((6,)), dma((6,)),
-            dma((8,)), dma((8,)),
-            dma((6,)), dma((6,)),
-            dma((6,)), dma((6,)),
+            dma((9,)), dma((9,)),
             dma((1,)), dma((1,)),
             dma((1,)), dma((1,)),
+            dma((1,)), dma((1,)),
+            dma((1,)), dma((4,)),
+            dma((1,)), dma((6,)),
         ],
         compiler_params=pltpu.CompilerParams(
             collective_id=0, has_side_effects=True, vmem_limit_bytes=60 * 1024 * 1024

time: 62.3 us -> 56 us (0.90)
  Pallas kernels: 61.4 us -> 55.1 us
    pallas_call x1, Pallas kernels: 61.4 us -> 55.1 us  [on_device(): pl.pallas_call(kernel, out_shape=pltpu.VMEM((1, 512, 768), BF16), in_spec...]
where the time goes in v3:
time: 56 us
  Pallas kernels  55.1 us (98%)
  local copies, waits for them, and re-layouts  0.88 us (2%)
    pallas_call x1, Pallas kernels, on_device(): pl.pallas_call(kernel, out_shape=pltpu.VMEM((1, 512, 768), BF16), in_spec...  55.1 us

profile of v3, /device:TPU:1, one launch (start us, length us, event | category | flops | bytes accessed | tf_op | source)
XLA Modules:
  0.0 56.0 jit_solution(6745476708818981770)
XLA Ops:
  0.0 55.1 %shard_map.82 = bf16[1,512,768]{2,1,0:T(8,128)(2,1)S(1)} custom-call(bf16[1,512,768]{2,1,0:T(8,128)(2,1)} %tok_h.1, bf16[1,512,768]{2,1,0:T(8,128)(2,1)} %og_h.1, bf16[1,512,1024]{2,1,0:T(8,128)(2,1)} %lg_h.1, bf16[64,768]{1,0:T(8,128)(2,1)} %bitcast.1, bf16[16,4,768]{2,1,0:T(4,128)(2,1)} %xin_h.1, bf16[1,64,768]{2,1,0:T(8,128)(2,1)} %so_h.1, ...), custom_call_target="tpu_custom_call" | custom-call | tf_op jit(solution)/shard_map/pallas_call | solution.py:515
  55.1 0.9 %copy.10 = bf16[1,512,768]{2,1,0:T(8,128)(2,1)} copy(bf16[1,512,768]{2,1,0:T(8,128)(2,1)S(1)} %shard_map.82) | data formatting | bytes 1572864

commit v4 on v3

--- a/solution.py
+++ b/solution.py
@@ -22,7 +22,7 @@
     tok_h, og_h, lg_h, pt_h, xin_h, so_h, win_h, wout_h, out_ref,
     lg, og, tok, win, wout, xin, cf, cb, pb, rp, hb, ry, st, qf, a2s, a2r, xf, gp, hc, b2s, b2r, zf, sp,
     ob, cc, dspf, lw, stl, s1b, s1l, s2b, dtl, dtb, acc, lgp, xp, xrp, hx, xry, xst, xq,
-    ld, cs_s, cs_r, y_s, y_r, a_s, a_r, b_s, b_r, g_s, g_r, k_s, k_r, o_s, o_r, p_s, p_r, s1_s, s1_r, s2_s, s2_r, dt_s, dt_r, xc_s, xc_r, x_s, x_r,
+    lg_s, ld, cs_s, cs_r, y_s, y_r, a_s, a_r, b_s, b_r, g_s, g_r, k_s, k_r, o_s, o_r, p_s, p_r, s1_s, s1_r, s2_s, s2_r, dt_s, dt_r, xc_s, xc_r, x_s, x_r,
 ):
     sgb, ptx = sp.at[0], sp.at[1].reshape(4, 2, 2, 4, 16, 768)
     c = lax.axis_index("clip")
@@ -41,6 +41,11 @@
     def rows_of(yy):
         return pl.ds(pl.multiple_of(yy * 16, 16), 16)
 
+    def drain(ref, sem):
+        pltpu.make_async_copy(ref, ref, sem).wait()
+
+    two = rp.at[pl.ds(0, 4)]
+
     def remote(src, dst, ssem, rsem, dev):
         return pltpu.make_async_remote_copy(
             src_ref=src, dst_ref=dst, send_sem=ssem, recv_sem=rsem, device_id=dev, device_id_type=MESH
@@ -63,7 +68,7 @@
         return (c, (s + i) % 16)
 
     loads = [
-        pltpu.make_async_copy(lg_h.at[0], lg, ld.at[0]),
+        None,
         pltpu.make_async_copy(og_h.at[0], og, ld.at[1]),
         pltpu.make_async_copy(so_h.at[0], ob.at[y, zl, h], ld.at[2]),
         pltpu.make_async_copy(pt_h.at[rows_of(x)], ptx.at[y, zl, h, x], ld.at[3]),
@@ -72,8 +77,12 @@
         pltpu.make_async_copy(wout_h.at[0], wout, ld.at[6]),
         pltpu.make_async_copy(tok_h.at[0], tok, ld.at[7]),
     ]
-    for load in loads:
+    lg_loads = [
+        pltpu.make_async_copy(lg_h.at[0, pl.ds(256 * i, 256)], lg.at[pl.ds(256 * i, 256)], lg_s.at[i]) for i in range(2)
+    ]
+    for load in lg_loads:
         load.start()
+    loads[1].start()
 
     barrier = pltpu.get_barrier_semaphore()
 
@@ -88,8 +97,6 @@
 
     to_plane(greet_plane)
     lax.fori_loop(0, 12, greet_group, 0)
-
-    loads[0].wait()
 
     def front(i, carry):
         rows = pl.ds(pl.multiple_of(i * 64, 64), 64)
@@ -100,7 +107,12 @@
         cb[rows, :] = comb.astype(BF16)
         return carry
 
-    lax.fori_loop(0, 8, front, 0, unroll=2)
+    for i in range(2):
+        lg_loads[i].wait()
+        lax.fori_loop(4 * i, 4 * i + 4, front, 0, unroll=2)
+        if i == 0:
+            for load in loads[2:]:
+                load.start()
     loads[1].wait()
 
     def cs_copy(i):
@@ -119,7 +131,7 @@
         cs_copy(i).start()
 
     def p_copy(i, ref, dev):
-        return remote(ref, ref, p_s.at[i], p_r.at[i], dev)
+        return remote(ref, ref, p_s.at[0], p_r.at[(0, 0, 0, 1, 2, 2, 3, 3, 4)[i]], dev)
 
     x_right, x_left = (xr * 4 + zh, s), (xl * 4 + zh, s)
     ps = [
@@ -148,7 +160,7 @@
     A, B = pl.ds(0, 8), pl.ds(8, 8)
 
     def y_copy(i, src, dev):
-        return remote(src, ry.at[i], y_s.at[i], y_r.at[i], dev)
+        return remote(src, ry.at[i], y_s.at[i // 2], y_r.at[(0, 1, 3, 2, 2, 3)[i]], dev)
 
     ys = [
         y_copy(0, hb.at[A, rows_of(y2)], right),
@@ -172,12 +184,11 @@
         return carry
 
     lax.fori_loop(0, 2, reorder, 0)
-    ys[0].wait_send()
-    ys[1].wait_send()
+    drain(two, y_s.at[0])
     ys[2].start()
     ys[3].start()
-    for i in range(3):
-        ps[i].wait_recv()
+    ptf = sp.at[1].reshape(64, 16, 768)
+    drain(ptf.at[pl.ds(0, 3)], p_r.at[0])
     ps[3].start()
     lax.fori_loop(2, 4, reorder, 0)
 
@@ -216,11 +227,11 @@
 
     def gather(buf, ss, rs):
         return [
-            remote(buf.at[y, :, h], buf.at[y, :, h], ss.at[1], rs.at[1], right),
-            remote(buf.at[y, :, h], buf.at[y, :, h], ss.at[2], rs.at[2], left),
-            remote(buf.at[yl, 0, h], buf.at[yl, 0, h], ss.at[3], rs.at[3], right),
-            remote(buf.at[yr, 1, h], buf.at[yr, 1, h], ss.at[4], rs.at[4], left),
-            remote(buf.at[:, :, h], buf.at[:, :, h], ss.at[5], rs.at[5], mate),
+            remote(buf.at[y, :, h], buf.at[y, :, h], ss.at[0], rs.at[1], right),
+            remote(buf.at[y, :, h], buf.at[y, :, h], ss.at[0], rs.at[1], left),
+            remote(buf.at[yl, 0, h], buf.at[yl, 0, h], ss.at[0], rs.at[2], right),
+            remote(buf.at[yr, 1, h], buf.at[yr, 1, h], ss.at[0], rs.at[2], left),
+            remote(buf.at[:, :, h], buf.at[:, :, h], ss.at[0], rs.at[3], mate),
         ]
 
     o_g = gather(ob, o_s, o_r)
@@ -246,16 +257,13 @@
     lax.fori_loop(1, 16, s2_start, 0)
     lax.fori_loop(3, 6, slope, 0)
 
-    ys[4].wait_send()
-    ys[5].wait_send()
+    drain(two, y_s.at[2])
     z_o.wait_recv()
     o_g[0].start()
     o_g[1].start()
-    ys[3].wait_recv()
-    ys[4].wait_recv()
+    drain(two, y_r.at[2])
     qf[0:8] = hb[A, rows_of(y), :].astype(F32) + ry[3].astype(F32) + ry[4].astype(F32)
-    ys[2].wait_recv()
-    ys[5].wait_recv()
+    drain(two, y_r.at[3])
     qf[8:16] = hb[B, rows_of(y), :].astype(F32) + ry[2].astype(F32) + ry[5].astype(F32)
     for i in range(4):
         a2s[:, i] = qf[:, 4 * i : 4 * i + 4, :].astype(BF16)
@@ -270,7 +278,7 @@
     pltpu.make_async_copy(s2b, s2b, s2_r.at[0]).wait()
 
     def xc_copy(i, k):
-        return remote(xp.at[k, :, other], xrp.at[k], xc_s.at[0], xc_r.at[i], mate)
+        return remote(xp.at[k, :, other], xrp.at[k], xc_s.at[0], xc_r.at[0], mate)
 
     def disp(i, carry):
         k = (y + 2 + i) % 4
@@ -284,22 +292,22 @@
 
     lax.fori_loop(0, 4, disp, 0)
 
-    o_g[0].wait_recv()
+    obf = ob.reshape(16, 64, 768)
+    drain(obf.at[pl.ds(0, 4)], o_r.at[1])
     o_g[2].start()
-    o_g[1].wait_recv()
     o_g[3].start()
 
     def x_half(i, carry):
         k = (y + 2 + i) % 4
-        xc_copy(i, k).wait_recv()
         hx[k] = (xp[k, :, mine].astype(F32) + xrp[k].astype(F32)).astype(BF16)
         return carry
 
+    drain(xrp, xc_r.at[0])
     lax.fori_loop(0, 4, x_half, 0)
     XA, XB = pl.ds(0, 128), pl.ds(128, 128)
 
     def x_copy(i, src, dev):
-        return remote(src, xry.at[i], x_s.at[0], x_r.at[i], dev)
+        return remote(src, xry.at[i], x_s.at[0], x_r.at[i // 2 if i < 2 else 1], dev)
 
     xs = [
         x_copy(0, hx.at[y2, XA], right),
@@ -311,9 +319,8 @@
     ]
     xs[0].start()
     xs[1].start()
-    ps[4].wait_recv()
+    drain(ptf.at[pl.ds(0, 16)], p_r.at[2])
     ps[6].start()
-    ps[5].wait_recv()
     ps[7].start()
 
     loads[6].wait()
@@ -334,8 +341,7 @@
     lax.fori_loop(0, 3, act, 0)
     xs[2].start()
     xs[3].start()
-    o_g[2].wait_recv()
-    o_g[3].wait_recv()
+    drain(obf.at[pl.ds(0, 2)], o_r.at[2])
     o_g[4].start()
 
     def grad(i, carry):
@@ -354,14 +360,12 @@
     pltpu.make_async_copy(b2s.at[c, h], b2r.at[c * 4 + q], b_r.at[0]).start()
     to_plane(b_start)
 
-    xs[0].wait_recv()
+    drain(two, x_r.at[0])
     xst[0] = (xry[0].astype(F32) + hx[yr, XA, :].astype(F32)).astype(BF16)
     xs[4].start()
-    xs[1].wait_recv()
     xst[1] = (xry[1].astype(F32) + hx[yl, XB, :].astype(F32)).astype(BF16)
     xs[5].start()
-    ps[6].wait_recv()
-    ps[7].wait_recv()
+    drain(ptf.at[pl.ds(0, 8)], p_r.at[3])
     ps[8].start()
     o_g[4].wait_recv()
 
@@ -390,8 +394,7 @@
         return carry
 
     lax.fori_loop(0, 3, comb_out, 0)
-    for i in range(2, 6):
-        xs[i].wait_recv()
+    drain(rp.at[pl.ds(0, 8)], x_r.at[1])
     xq[XA, :] = hx[y, XA, :].astype(F32) + xry[3].astype(F32) + xry[4].astype(F32)
     xq[XB, :] = hx[y, XB, :].astype(F32) + xry[2].astype(F32) + xry[5].astype(F32)
 
@@ -403,11 +406,11 @@
 
     def g_copy(i, part, yy, dev):
         ref = sgb.at[part, rows_of(yy), mine]
-        return remote(ref, ref, g_s.at[min(i, 2)], g_r.at[i], dev)
+        return remote(ref, ref, g_s.at[min(i // 2, 1)], g_r.at[(0, 1, 2, 2, 3, 3)[i]], dev)
 
     def k_copy(i, part, yy):
         ref = sgb.at[part, rows_of(yy), mine]
-        return remote(ref, ref, k_s.at[0], k_r.at[i], mate)
+        return remote(ref, ref, k_s.at[0], k_r.at[(0, 0, 1, 2, 1, 2, 3, 3)[i]], mate)
 
     gs = [
         g_copy(0, A, y, right),
@@ -447,8 +450,7 @@
         return carry
 
     lax.fori_loop(1, 16, dt_start, 0)
-    gs[0].wait_send()
-    gs[1].wait_send()
+    drain(two, g_s.at[0])
     gs[2].start()
     gs[3].start()
     gs[0].wait_recv()
@@ -459,48 +461,41 @@
     ks[3].start()
     pltpu.make_async_copy(dtb, dtb, dt_r.at[0]).wait()
 
-    def use(yy):
+    def prepare(yy):
         w = sgb[:, rows_of(yy), :].reshape(256, 768)
         d = lax.dot_general(tok[...], w, NT, preferred_element_type=F32)
         lw[yy, :, 256:512] = (dspf[yy] * (d - jnp.sum(dtb[pl.ds(yy * 4, 4)], axis=0))).astype(BF16)
-        both = sp[:, :, rows_of(yy), :].reshape(512, 768)
-        return jnp.dot(lw[yy], both, preferred_element_type=F32)
-
-    def add(yy):
-        acc[...] += use(yy)
-
-    ks[0].wait_recv()
-    ks[1].wait_recv()
-    add(y)
-    gs[2].wait_recv()
+
+    def use(yy):
+        return jnp.dot(lw[yy], sp[:, :, rows_of(yy), :].reshape(512, 768), preferred_element_type=F32)
+
+    drain(two, k_r.at[0])
+    prepare(y)
+    acc[...] += use(y)
+    drain(two, g_r.at[2])
     ks[4].start()
-    gs[3].wait_recv()
     ks[5].start()
-    ks[2].wait_recv()
-    ks[4].wait_recv()
-    add(yl)
-    gs[4].wait_recv()
+    drain(two, k_r.at[1])
+    prepare(yl)
+    drain(two, g_r.at[3])
     ks[6].start()
-    gs[5].wait_recv()
     ks[7].start()
-    ks[3].wait_recv()
-    ks[5].wait_recv()
-    add(yr)
-    ks[6].wait_recv()
-    ks[7].wait_recv()
+    acc[...] += use(yl)
+    drain(two, k_r.at[2])
+    prepare(yr)
+    acc[...] += use(yr)
+    drain(two, k_r.at[3])
+    prepare(y2)
     out_ref[0] = (acc[...] + use(y2)).astype(BF16)
 
-    for copy in ys[2:4] + o_g + ps + [z_o]:
-        copy.wait_send()
-
-    def drain(buf_src, sem):
-        pltpu.make_async_copy(buf_src, buf_src, sem).wait()
-
+    drain(two, y_s.at[1])
+    drain(obf.at[pl.ds(0, 15)], o_s.at[0])
+    drain(ptf.at[pl.ds(0, 63)], p_s.at[0])
     drain(rp, cs_s.at[0])
     drain(rp, xc_s.at[0])
     drain(rp, k_s.at[0])
     drain(rp.at[pl.ds(0, 12)], x_s.at[0])
-    drain(rp.at[pl.ds(0, 8)], g_s.at[2])
+    drain(rp.at[pl.ds(0, 8)], g_s.at[1])
     drain(a2r.at[pl.ds(0, 63)], a_s.at[0])
     drain(b2r.at[pl.ds(0, 63)], b_s.at[0])
     drain(s1b.at[pl.ds(0, 3)], s1_s.at[0])
@@ -559,20 +554,20 @@
             vm((6, 128, 384), BF16),
             vm((2, 128, 384), BF16),
             vm((256, 384), F32),
-            dma((8,)),
+            dma((2,)), dma((8,)),
             dma((1,)), dma((4,)),
-            dma((6,)), dma((6,)),
+            dma((3,)), dma((4,)),
             dma((1,)), dma((1,)),
             dma((1,)), dma((1,)),
-            dma((3,)), dma((6,)),
-            dma((1,)), dma((8,)),
-            dma((6,)), dma((6,)),
-            dma((9,)), dma((9,)),
+            dma((2,)), dma((4,)),
+            dma((1,)), dma((4,)),
+            dma((1,)), dma((4,)),
+            dma((1,)), dma((5,)),
             dma((1,)), dma((1,)),
             dma((1,)), dma((1,)),
             dma((1,)), dma((1,)),
-            dma((1,)), dma((4,)),
-            dma((1,)), dma((6,)),
+            dma((1,)), dma((1,)),
+            dma((1,)), dma((2,)),
         ],
         compiler_params=pltpu.CompilerParams(
             collective_id=0, has_side_effects=True, vmem_limit_bytes=60 * 1024 * 1024

time: 56 us -> 55.7 us (level)
  no operation moved by 1% of the time
where the time goes in v4:
time: 55.7 us; the launch traced here: 55.6 us
  Pallas kernels  54.7 us (98%)
  local copies, waits for them, and re-layouts  0.88 us (2%)
    pallas_call x1, Pallas kernels, on_device(): pl.pallas_call(kernel, out_shape=pltpu.VMEM((1, 512, 768), BF16), in_spec...  54.7 us

profile of v4, /device:TPU:1, one launch (start us, length us, event | category | flops | bytes accessed | tf_op | source)
XLA Modules:
  0.0 55.6 jit_solution(2866453965363587210)
XLA Ops:
  0.0 54.7 %shard_map.82 = bf16[1,512,768]{2,1,0:T(8,128)(2,1)S(1)} custom-call(bf16[1,512,768]{2,1,0:T(8,128)(2,1)} %tok_h.1, bf16[1,512,768]{2,1,0:T(8,128)(2,1)} %og_h.1, bf16[1,512,1024]{2,1,0:T(8,128)(2,1)} %lg_h.1, bf16[64,768]{1,0:T(8,128)(2,1)} %bitcast.1, bf16[16,4,768]{2,1,0:T(4,128)(2,1)} %xin_h.1, bf16[1,64,768]{2,1,0:T(8,128)(2,1)} %so_h.1, ...), custom_call_target="tpu_custom_call" | custom-call | tf_op jit(solution)/shard_map/pallas_call | solution.py:510
  54.8 0.9 %copy.10 = bf16[1,512,768]{2,1,0:T(8,128)(2,1)} copy(bf16[1,512,768]{2,1,0:T(8,128)(2,1)S(1)} %shard_map.82) | data formatting | bytes 1572864

commit v5 on v4

--- a/solution.py
+++ b/solution.py
@@ -21,7 +21,7 @@
 def kernel(
     tok_h, og_h, lg_h, pt_h, xin_h, so_h, win_h, wout_h, out_ref,
     lg, og, tok, win, wout, xin, cf, cb, pb, rp, hb, ry, st, qf, a2s, a2r, xf, gp, hc, b2s, b2r, zf, sp,
-    ob, cc, dspf, lw, stl, s1b, s1l, s2b, dtl, dtb, acc, lgp, xp, xrp, hx, xry, xst, xq,
+    ob, cc, dspf, lw, stl, s1b, s1l, s2b, dtl, dtb, acc, lgp, xp, xrp, hx, xry, xst, xq, dn,
     lg_s, ld, cs_s, cs_r, y_s, y_r, a_s, a_r, b_s, b_r, g_s, g_r, k_s, k_r, o_s, o_r, p_s, p_r, s1_s, s1_r, s2_s, s2_r, dt_s, dt_r, xc_s, xc_r, x_s, x_r,
 ):
     sgb, ptx = sp.at[0], sp.at[1].reshape(4, 2, 2, 4, 16, 768)
@@ -75,7 +75,7 @@
         pltpu.make_async_copy(xin_h, xin, ld.at[4]),
         pltpu.make_async_copy(win_h.at[0], win, ld.at[5]),
         pltpu.make_async_copy(wout_h.at[0], wout, ld.at[6]),
-        pltpu.make_async_copy(tok_h.at[0], tok, ld.at[7]),
+        pltpu.make_async_copy(tok_h.at[0], tok, ld.at[0]),
     ]
     lg_loads = [
         pltpu.make_async_copy(lg_h.at[0, pl.ds(256 * i, 256)], lg.at[pl.ds(256 * i, 256)], lg_s.at[i]) for i in range(2)
@@ -341,8 +341,6 @@
     lax.fori_loop(0, 3, act, 0)
     xs[2].start()
     xs[3].start()
-    drain(obf.at[pl.ds(0, 2)], o_r.at[2])
-    o_g[4].start()
 
     def grad(i, carry):
         part = pl.ds(pl.multiple_of(i * 256, 256), 256)
@@ -360,6 +358,8 @@
     pltpu.make_async_copy(b2s.at[c, h], b2r.at[c * 4 + q], b_r.at[0]).start()
     to_plane(b_start)
 
+    drain(obf.at[pl.ds(0, 2)], o_r.at[2])
+    o_g[4].start()
     drain(two, x_r.at[0])
     xst[0] = (xry[0].astype(F32) + hx[yr, XA, :].astype(F32)).astype(BF16)
     xs[4].start()
@@ -461,9 +461,16 @@
     ks[3].start()
     pltpu.make_async_copy(dtb, dtb, dt_r.at[0]).wait()
 
-    def prepare(yy):
-        w = sgb[:, rows_of(yy), :].reshape(256, 768)
-        d = lax.dot_general(tok[...], w, NT, preferred_element_type=F32)
+    def columns(yy, half):
+        w = sgb[:, rows_of(yy), half].reshape(256, 384)
+        return lax.dot_general(tok[:, half], w, NT, preferred_element_type=F32)
+
+    def prepare(yy, begun=None):
+        if begun is None:
+            w = sgb[:, rows_of(yy), :].reshape(256, 768)
+            d = lax.dot_general(tok[...], w, NT, preferred_element_type=F32)
+        else:
+            d = begun[...] + columns(yy, other)
         lw[yy, :, 256:512] = (dspf[yy] * (d - jnp.sum(dtb[pl.ds(yy * 4, 4)], axis=0))).astype(BF16)
 
     def use(yy):
@@ -475,14 +482,16 @@
     drain(two, g_r.at[2])
     ks[4].start()
     ks[5].start()
+    dn[0] = columns(yl, mine)
+    dn[1] = columns(yr, mine)
     drain(two, k_r.at[1])
-    prepare(yl)
+    prepare(yl, dn.at[0])
+    drain(two, k_r.at[2])
+    prepare(yr, dn.at[1])
     drain(two, g_r.at[3])
     ks[6].start()
     ks[7].start()
     acc[...] += use(yl)
-    drain(two, k_r.at[2])
-    prepare(yr)
     acc[...] += use(yr)
     drain(two, k_r.at[3])
     prepare(y2)
@@ -554,7 +563,8 @@
             vm((6, 128, 384), BF16),
             vm((2, 128, 384), BF16),
             vm((256, 384), F32),
-            dma((2,)), dma((8,)),
+            vm((2, 512, 256), F32),
+            dma((2,)), dma((7,)),
             dma((1,)), dma((4,)),
             dma((3,)), dma((4,)),
             dma((1,)), dma((1,)),

time: 55.7 us -> 55.3 us (level)
  no operation moved by 1% of the time
where the time goes in v5:
time: 55.3 us; the launch traced here: 55.2 us
  Pallas kernels  54.4 us (98%)
  local copies, waits for them, and re-layouts  0.88 us (2%)
    pallas_call x1, Pallas kernels, on_device(): pl.pallas_call(kernel, out_shape=pltpu.VMEM((1, 512, 768), BF16), in_spec...  54.4 us

profile of v5, /device:TPU:1, one launch (start us, length us, event | category | flops | bytes accessed | tf_op | source)
XLA Modules:
  0.0 55.2 jit_solution(12527813673135544237)
XLA Ops:
  0.0 54.4 %shard_map.82 = bf16[1,512,768]{2,1,0:T(8,128)(2,1)S(1)} custom-call(bf16[1,512,768]{2,1,0:T(8,128)(2,1)} %tok_h.1, bf16[1,512,768]{2,1,0:T(8,128)(2,1)} %og_h.1, bf16[1,512,1024]{2,1,0:T(8,128)(2,1)} %lg_h.1, bf16[64,768]{1,0:T(8,128)(2,1)} %bitcast.1, bf16[16,4,768]{2,1,0:T(4,128)(2,1)} %xin_h.1, bf16[1,64,768]{2,1,0:T(8,128)(2,1)} %so_h.1, ...), custom_call_target="tpu_custom_call" | custom-call | tf_op jit(solution)/shard_map/pallas_call | solution.py:519
  54.4 0.9 %copy.10 = bf16[1,512,768]{2,1,0:T(8,128)(2,1)} copy(bf16[1,512,768]{2,1,0:T(8,128)(2,1)S(1)} %shard_map.82) | data formatting | bytes 1572864
